TPU v7x, 256 devices: a whole 4x4x8 slice. The times are simulated.
256 devices in a mesh: lat: 4 (over z_lo), wave: 64 (over z_hi, y, x, core).
Axes of the slice: x: 4, y: 4, z: 8 (z_hi: 2, z_lo: 4; z = z_hi * 4 + z_lo), core: 2. Of those that a mesh axis runs over, the one named last changes fastest.
Arguments:
- fourier: bfloat16 [2, 1024, 1024, 128], P(None, ('lat', 'wave')), may hold values from -6 to 6
- cycle_points: int32 [1024], P(('lat', 'wave')), may hold values from 20 to 4120, as said below
- wave_table: int32 [1024], replicated, may hold values from 0 to 1023, as said below
- legendre: bfloat16 [1024, 1024, 1024], P('wave', 'lat'), as said below
Outputs:
- spectral: bfloat16 [1024, 1024, 128], P('wave', 'lat')
Inputs may be any that keep to these rules, and one draw needn't show every extreme that they name: wave_table is a permutation of 0 to 1023; slots 16 q to 16 q + 15 hold 16 consecutive wavenumbers in rising order. legendre[r, k, l] is zero wherever the degree wave_table[r] + 2 j + p exceeds 1024 - 1, with p = 1 if l >= 512 else 0 and j = l - p * 512. `cycle_points`: cycle k has about 4 k + 20 points.
All inputs are finite; a program needn't handle non-finite values.
Results may differ from a plain program's by a relative error of at most 0.0085.
Values may be sent and summed in bfloat16 or wider, within the bound.
No kernel may reach another device: no remote copies, remote signals or barrier semaphores. Data moves between devices by JAX's collectives and lax.ppermute only.
A program may use at most 128 MiB of HBM per device.

v0:
```python
import jax
import jax.numpy as jnp
from jax import lax
from jax.sharding import PartitionSpec as P


def contract(piece, inputs, bands):
    slots, cycles, columns = piece.shape
    cycle_band = cycles // bands
    left = piece.reshape(slots, bands, cycle_band, columns)
    right = inputs.reshape(bands, cycle_band, inputs.shape[1], inputs.shape[2])
    parts = jnp.einsum("mbkl,bkmc->bmlc", left, right, preferred_element_type=jnp.float32)
    return jnp.sum(parts.astype(jnp.bfloat16).astype(jnp.float32), axis=0)


def project(legendre, inputs, bands):
    return contract(legendre, inputs, bands)


def per_device(fourier, cycle_points, wave_table, legendre):
    waves_all = wave_table.shape[0]
    half = waves_all // 2
    waves = jnp.arange(waves_all, dtype=jnp.int32)
    present = (2 * waves[None, :] < cycle_points[:, None]).astype(jnp.bfloat16)
    kept = fourier * present[None, :, :, None]
    ordered = jnp.take(kept, wave_table, axis=2)
    banded = lax.all_to_all(ordered, "wave", split_axis=2, concat_axis=1, tiled=True)
    north = banded[0].astype(jnp.float32)
    south = banded[1].astype(jnp.float32)
    even_part = (north + south).astype(jnp.bfloat16)
    odd_part = (north - south).astype(jnp.bfloat16)
    moved = lax.all_to_all(legendre, "lat", split_axis=2, concat_axis=1, tiled=True)
    block_cols = moved.shape[2]
    first_col = lax.axis_index("lat") * block_cols
    parity = (first_col >= half).astype(jnp.int32)
    even_all, odd_all = (
        lax.all_gather(even_part, "lat", axis=0, tiled=True),
        lax.all_gather(odd_part, "lat", axis=0, tiled=True),
    )
    gathered = jnp.where(parity == 1, odd_all, even_all)
    result = project(moved, gathered, lax.axis_size("lat"))
    return result.astype(jnp.bfloat16)


def solution(mesh):
    placed = (P(None, ("lat", "wave"), None, None), P(("lat", "wave")), P(), P("wave", "lat", None))
    return jax.shard_map(
        per_device, mesh=mesh, in_specs=placed, out_specs=P("wave", "lat", None), check_vma=False
    )
```

profile of v0, /device:TPU:1, one launch (start us, length us, event | category | flops | bytes accessed | tf_op | source)
XLA Modules:
  0.0 455.1 jit_solution(8741149732136601205)
XLA Ops:
  6.5 0.0 all-gather.3.cloned.1.call-start
  6.5 0.7 fusion.9
  7.2 0.7 compare_and_fusion
  7.9 0.7 compare_convert_fusion
  8.7 0.2 copy.17
  8.9 4.6 %copy_multiply_fusion = bf16[2,4,1024,128]{3,1,2,0:T(4,128)(2,1)} fusion(bf16[2,4,1024,128]{3,2,1,0:T(8,128)(2,1)} %param.4, bf16[4,1024]{0,1:T(8,128)(2,1)S(1)} %copy.17), kind=kLoop, calls=%fused_computation.11 | loop fusion | flops 1048576 | bytes 4202496 | tf_op jit(solution)/shard_map/mul | solution.py:25
  13.4 6.0 %gather_fusion = bf16[1024,2,4,128]{3,2,1,0:T(4,128)(2,1)S(1)} fusion(bf16[2,4,1024,128]{3,1,2,0:T(4,128)(2,1)} %copy_multiply_fusion, s32[1024]{0:T(1024)S(1)} %fusion.9), kind=kCustom, calls=%fused_computation | custom fusion | bytes 4198400 | tf_op jit(solution)/shard_map/jit(_take)/gather | solution.py:26
  19.5 3.8 select_bitcast_fusion
  23.3 53.2 %all_to_all.30 = bf16[2,4,1024,128]{3,1,0,2:T(4,128)(2,1)S(1)} all-to-all(bf16[2,4,1024,128]{3,1,0,2:T(4,128)(2,1)S(1)} %select_bitcast_fusion), channel_id=1, replica_groups=mesh['lat'=4,'wave'=64] {'wave'}, dimensions={2} | all-to-all | bytes 4194304 | tf_op jit(solution)/shard_map/all_to_all | solution.py:27
  76.5 0.6 copy.33
  77.2 1.9 fusion.8
  79.1 0.0 all-gather.3.cloned.1.call-update
  79.1 12.6 %copy.20 = bf16[16,256,1024]{1,0,2:T(8,128)(2,1)} copy(bf16[16,256,1024]{2,1,0:T(8,128)(2,1)} %param.7) | data formatting | bytes 16777216 | tf_op args[3]
  91.7 18.9 %all-to-all-start.1 = ((bf16[16,256,1024]{1,0,2:T(8,128)(2,1)}), bf16[16,256,1024]{1,0,2:T(8,128)(2,1)}, u32[]{:S(2)}, u32[]{:S(2)}) async-start(bf16[16,256,1024]{1,0,2:T(8,128)(2,1)} %copy.20), calls=%async_computation.1 | async-start | bytes 16777216 | tf_op jit(solution)/shard_map/all_to_all | solution.py:32
  110.6 0.0 all-gather.5.cloned.1.call-start
  110.6 0.7 all-gather.5.cloned.1.call-update
  111.3 136.6 %all-gather.3.cloned.1.call-done = bf16[1024,16,128]{2,1,0:T(8,128)(2,1)} async-done(((bf16[256,16,128]{2,1,0:T(8,128)(2,1)}), bf16[1024,16,128]{2,1,0:T(8,128)(2,1)}) %all-gather.3.cloned.1.call-update) | async-done | bytes 4194320 | tf_op jit(solution)/shard_map/all_gather | solution.py:38
  247.9 174.3 %all-gather.5.cloned.1.call-done = bf16[1024,16,128]{2,1,0:T(8,128)(2,1)} async-done(((bf16[256,16,128]{2,1,0:T(8,128)(2,1)}), bf16[1024,16,128]{2,1,0:T(8,128)(2,1)}) %all-gather.5.cloned.1.call-update) | async-done | bytes 4194320 | tf_op jit(solution)/shard_map/all_gather | solution.py:37
  422.2 4.6 %broadcast_select_fusion = bf16[1024,16,128]{2,1,0:T(8,128)(2,1)} fusion(bf16[1024,16,128]{2,1,0:T(8,128)(2,1)} %all-gather.3.cloned.1.call-done, bf16[1024,16,128]{2,1,0:T(8,128)(2,1)} %all-gather.5.cloned.1.call-done, pred[]{:T(512)S(6)} %eq.3), kind=kLoop, calls=%fused_computation.5 | loop fusion | flops 2097152 | bytes 12582913 | tf_op jit(solution)/shard_map/jit(_where)/select_n | solution.py:40
  426.8 0.0 all-to-all-done.1
  426.8 13.8 %copy.22 = bf16[16,256,4,256]{3,1,0,2:T(8,128)(2,1)} copy(bf16[16,256,4,256]{1,0,3,2:T(8,128)(2,1)} %bitcast.6) | data formatting | bytes 16777216 | tf_op jit(solution)/shard_map/all_to_all | solution.py:32
  440.6 6.3 %convert_reduce_fusion = bf16[16,128,256]{2,1,0:T(8,128)(2,1)S(1)} fusion(bf16[16,256,4,256]{3,1,0,2:T(8,128)(2,1)} %copy.22, bf16[4,256,16,128]{3,2,1,0:T(8,128)(2,1)} %bitcast.18), kind=kOutput, calls=%fused_computation.4 | convolution fusion | flops 1077411840 | bytes 13631488 | tf_op jit(solution)/shard_map/mbkl,bkmc->bmlc/dot_general | solution.py:12
  446.9 1.3 copy.24
  (1 shorter events, 0.0 us)
Async XLA Ops:
  6.5 241.4 %all-gather.3.cloned.1.call-start = ((), (), s32[]{:S(2)}) async-start(), calls=%async_computation.2 | async-start | bytes 5242880 | tf_op jit(solution)/shard_map/all_gather | solution.py:38
  91.7 335.1 %all-to-all-start.1 = ((bf16[16,256,1024]{1,0,2:T(8,128)(2,1)}), bf16[16,256,1024]{1,0,2:T(8,128)(2,1)}, u32[]{:S(2)}, u32[]{:S(2)}) async-start(bf16[16,256,1024]{1,0,2:T(8,128)(2,1)} %copy.20), calls=%async_computation.1 | async-start | bytes 16777216 | tf_op jit(solution)/shard_map/all_to_all | solution.py:32
  110.6 311.6 %all-gather.5.cloned.1.call-start = ((), (), s32[]{:S(2)}) async-start(), calls=%async_computation.3 | async-start | bytes 5242880 | tf_op jit(solution)/shard_map/all_gather | solution.py:37
Sparse Core Ops, SparseCore 0:
  79.2 168.6 all-gather.2
  249.7 172.4 all-gather.4
where the time goes:
time: 456 us; the launch traced here: 455 us
  waiting for transfers between devices  312 us (68%)
  blocking collectives  53.2 us (12%)
  local copies, waits for them, and re-layouts  34.6 us (8%)
  starting transfers between devices  18.9 us (4%)
  other arithmetic  17 us (4%)
  between operations  13.4 us (3%)
  matrix products  6.34 us (1%)
    all_gather x1, waiting for transfers between devices, per_device(): lax.all_gather(even_part, 'lat', axis=0, tiled=True)  174 us
    all_gather x1, waiting for transfers between devices, per_device(): lax.all_gather(odd_part, 'lat', axis=0, tiled=True)  137 us
    all_to_all x1, blocking collectives, per_device(): lax.all_to_all(ordered, 'wave', split_axis=2, concat_axis=1, tiled=True)  53.2 us
    all_to_all x1, starting transfers between devices, per_device(): lax.all_to_all(legendre, 'lat', split_axis=2, concat_axis=1, tiled=True)  18.9 us
    all_to_all x1, local copies, waits for them, and re-layouts, per_device(): lax.all_to_all(legendre, 'lat', split_axis=2, concat_axis=1, tiled=True)  13.8 us
    unnamed x1, local copies, waits for them, and re-layouts  12.6 us
  transfers between devices with their start and end apart: 3, of which 2 were waited for; matrix products, arithmetic and copies ran while one was open for 4% of the time, Pallas kernels for 0%

commit v1 on v0

v1 whole, which is shorter than its diff:
```python
import functools

import jax
import jax.numpy as jnp
from jax import lax
from jax.experimental import pallas as pl
from jax.experimental.pallas import tpu as pltpu
from jax.sharding import PartitionSpec as P


def parts_kernel(groups, width, points_ref, table_ref, fourier_ref, out_ref):
    cycles = fourier_ref.shape[1]
    channels = fourier_ref.shape[3]

    @pl.loop(0, groups)
    def _(q):
        first = pl.multiple_of(table_ref[q * width] // width * width, width)
        for k in range(cycles):
            wave = first + lax.broadcasted_iota(jnp.int32, (width, channels), 0)
            keep = 2 * wave < points_ref[k]
            north = fourier_ref[0, k, pl.ds(first, width), :].astype(jnp.float32)
            south = fourier_ref[1, k, pl.ds(first, width), :].astype(jnp.float32)
            out_ref[q, 0, k] = jnp.where(keep, north + south, 0.0).astype(out_ref.dtype)
            out_ref[q, 1, k] = jnp.where(keep, north - south, 0.0).astype(out_ref.dtype)


def make_parts(fourier, cycle_points, wave_table, groups):
    _, cycles, waves, channels = fourier.shape
    width = waves // groups
    return pl.pallas_call(
        functools.partial(parts_kernel, groups, width),
        out_shape=jax.ShapeDtypeStruct((groups, 2, cycles, width, channels), fourier.dtype),
        in_specs=[
            pl.BlockSpec(memory_space=pltpu.SMEM),
            pl.BlockSpec(memory_space=pltpu.SMEM),
            pl.BlockSpec(memory_space=pltpu.VMEM),
        ],
        out_specs=pl.BlockSpec(memory_space=pltpu.VMEM),
        name="make_parts",
    )(cycle_points, wave_table, fourier)


def band_kernel(parts_ref, legendre_ref, out_ref):
    blocks, _, _, cols = out_ref.shape
    half = blocks // 2
    for b in range(blocks):
        part = parts_ref[b // half, 0]
        piece = legendre_ref[0, :, b * cols : (b + 1) * cols]
        total = lax.dot_general(part, piece, (((0,), (0,)), ((), ())), preferred_element_type=jnp.float32)
        out_ref[b, 0] = total.astype(out_ref.dtype)


def band_sums(parts, legendre, blocks):
    _, slots, cycles, channels = parts.shape
    columns = legendre.shape[2]
    cols = columns // blocks
    return pl.pallas_call(
        band_kernel,
        grid=(slots,),
        out_shape=jax.ShapeDtypeStruct((blocks, slots, channels, cols), parts.dtype),
        in_specs=[
            pl.BlockSpec((2, 1, cycles, channels), lambda m: (0, m, 0, 0)),
            pl.BlockSpec((1, cycles, columns), lambda m: (m, 0, 0)),
        ],
        out_specs=pl.BlockSpec((blocks, 1, channels, cols), lambda m: (0, m, 0, 0)),
        name="band_sums",
    )(parts, legendre)


def per_device(fourier, cycle_points, wave_table, legendre):
    groups = lax.axis_size("wave")
    bands = lax.axis_size("lat")
    sent = make_parts(fourier, cycle_points, wave_table, groups)
    got = lax.all_to_all(sent, "wave", split_axis=0, concat_axis=0, tiled=True)
    _, _, cycles, width, channels = got.shape
    parts = jnp.transpose(got, (1, 3, 0, 2, 4)).reshape(2, width, groups * cycles, channels)
    sums = band_sums(parts, legendre, bands)
    moved = lax.all_to_all(sums, "lat", split_axis=0, concat_axis=0, tiled=True)
    total = jnp.sum(moved.astype(jnp.float32), axis=0).astype(jnp.bfloat16)
    return jnp.transpose(total, (0, 2, 1))


def solution(mesh):
    placed = (P(None, ("lat", "wave"), None, None), P(("lat", "wave")), P(), P("wave", "lat", None))
    return jax.shard_map(
        per_device, mesh=mesh, in_specs=placed, out_specs=P("wave", "lat", None), check_vma=False
    )
```

time: 456 us -> 192 us (0.42)
  waiting for transfers between devices: 312 us -> 0 us
  blocking collectives: 53.2 us -> 167 us
  local copies, waits for them, and re-layouts: 34.6 us -> 3.77 us
  starting transfers between devices: 18.9 us -> 0 us
  Pallas kernels: 0 us -> 17.8 us
  other arithmetic: 17 us -> 3.08 us
  between operations: 13.4 us -> 0.01 us
  matrix products: 6.34 us -> 0 us
    all_gather x2 -> x0, waiting for transfers between devices: 311 us -> none  [the longest x1 174 us: per_device(): lax.all_gather(even_part, 'lat', axis=0, tiled=True)]
    all_to_all x1 -> x2, blocking collectives: 53.2 us -> 167 us  [the longest x1 114 us: per_device(): moved = lax.all_to_all(sums, 'lat', split_axis=0, concat_axis=0, tiled=True)]
    all_to_all x1 -> x0, starting transfers between devices: 18.9 us -> none  [per_device(): lax.all_to_all(legendre, 'lat', split_axis=2, concat_axis=1, tiled=True)]
    pallas_call x0 -> x2, Pallas kernels: none -> 17.8 us  [the longest x1 13.3 us: band_sums(): pl.pallas_call(band_kernel, grid=(slots,), out_shape=jax.ShapeDtypeStruct...]
    all_to_all x2 -> x0, local copies, waits for them, and re-layouts: 14.4 us -> none  [the longest x1 13.8 us: per_device(): lax.all_to_all(legendre, 'lat', split_axis=2, concat_axis=1, tiled=True)]
    unnamed x1 -> x0, local copies, waits for them, and re-layouts: 12.6 us -> none
    select_n x2 -> x0, other arithmetic: 8.42 us -> none  [the longest x1 4.59 us: per_device(): gathered = jnp.where(parity == 1, odd_all, even_all)]
    dot_general x1 -> x0, matrix products: 6.34 us -> none  [contract(): jnp.einsum('mbkl,bkmc->bmlc', left, right, preferred_element_type=jnp.flo...]
  transfers between devices with their start and end apart: 3 -> 0, of which waited for: 2 -> 0; matrix products, arithmetic and copies ran while one was open for 4% -> 0% of each run, Pallas kernels for 0% -> 0%
where the time goes in v1:
time: 192 us
  blocking collectives  167 us (87%)
  Pallas kernels  17.8 us (9%)
  local copies, waits for them, and re-layouts  3.77 us (2%)
  other arithmetic  3.08 us (2%)
    all_to_all x1, blocking collectives, per_device(): moved = lax.all_to_all(sums, 'lat', split_axis=0, concat_axis=0, tiled=True)  114 us
    all_to_all x1, blocking collectives, per_device(): got = lax.all_to_all(sent, 'wave', split_axis=0, concat_axis=0, tiled=True)  53.4 us
    pallas_call x1, Pallas kernels, band_sums(): pl.pallas_call(band_kernel, grid=(slots,), out_shape=jax.ShapeDtypeStruct...  13.3 us
    pallas_call x1, Pallas kernels, make_parts(): pl.pallas_call(functools.partial(parts_kernel, groups, width), out_shape=...  4.43 us

profile of v1, /device:TPU:1, one launch (start us, length us, event | category | flops | bytes accessed | tf_op | source)
XLA Modules:
  0.0 191.7 jit_solution(2472237517521479203)
XLA Ops:
  0.0 4.4 %make_parts.1 = bf16[64,2,4,16,128]{4,3,2,1,0:T(8,128)(2,1)} custom-call(s32[4]{0:T(128)} %points_ref.1, s32[1024]{0:T(1024)} %table_ref.1, bf16[2,4,1024,128]{3,2,1,0:T(8,128)(2,1)} %fourier_ref.1), custom_call_target="tpu_custom_call" | custom-call | tf_op jit(solution)/shard_map/make_parts/pallas_call | solution.py:30
  4.4 53.4 %all_to_all.10 = bf16[64,2,4,16,128]{4,3,2,1,0:T(8,128)(2,1)S(1)} all-to-all(bf16[64,2,4,16,128]{4,3,2,1,0:T(8,128)(2,1)} %make_parts.1), channel_id=1, replica_groups=mesh['lat'=4,'wave'=64] {'wave'}, dimensions={0} | all-to-all | bytes 4194304 | tf_op jit(solution)/shard_map/all_to_all | solution.py:74
  57.9 2.5 %copy.6 = bf16[2,16,64,4,128]{4,3,2,1,0:T(4,128)(2,1)} copy(bf16[2,16,64,4,128]{4,1,3,0,2:T(8,128)(2,1)S(1)} %bitcast.4) | data formatting | bytes 4194304 | tf_op jit(solution)/shard_map/transpose | solution.py:76
  60.3 13.3 %band_sums.1 = bf16[4,16,128,256]{3,2,1,0:T(8,128)(2,1)} custom-call(bf16[2,16,256,128]{3,2,1,0:T(8,128)(2,1)} %bitcast.3, bf16[16,256,1024]{2,1,0:T(8,128)(2,1)} %legendre_ref.1), custom_call_target="tpu_custom_call" | custom-call | tf_op jit(solution)/shard_map/band_sums/pallas_call | solution.py:57
  73.7 113.7 %all_to_all.11 = bf16[4,16,128,256]{3,2,1,0:T(8,128)(2,1)} all-to-all(bf16[4,16,128,256]{3,2,1,0:T(8,128)(2,1)} %band_sums.1), channel_id=1, replica_groups=mesh['lat'=4,'wave'=64] {'lat'}, dimensions={0} | all-to-all | bytes 8388608 | tf_op jit(solution)/shard_map/all_to_all | solution.py:78
  187.3 3.1 %reduce_sum.12 = bf16[16,128,256]{2,1,0:T(8,128)(2,1)S(1)} reduce(bf16[4,16,128,256]{3,2,1,0:T(8,128)(2,1)} %all_to_all.11, bf16[]{:T(256)} %constant.2.clone.1), dimensions={0}, to_apply=%region_0.0 | reduce | flops 1572864 | bytes 5242882 | tf_op jit(solution)/shard_map/reduce_sum | solution.py:79
  190.4 1.3 copy.7

commit v2 on v1

v2 whole, which is shorter than its diff:
```python
import functools

import jax
import jax.numpy as jnp
from jax import lax
from jax.experimental import pallas as pl
from jax.experimental.pallas import tpu as pltpu
from jax.sharding import PartitionSpec as P

CHUNKS = (4,4,4,4)
FINISH_BYTES = 8000000
LATE = True


def parts_kernel(groups, width, points_ref, table_ref, fourier_ref, out_ref):
    cycles = fourier_ref.shape[1]
    channels = fourier_ref.shape[3]
    row = lax.broadcasted_iota(jnp.int32, (width, channels), 0)

    @pl.loop(0, groups, unroll=2)
    def _(q):
        first = pl.multiple_of(table_ref[q * width] // width * width, width)
        rows = pl.ds(first, width)
        for k in range(cycles):
            keep = row < (points_ref[k] + 1) // 2 - first
            north = fourier_ref[0, k, rows, :].astype(jnp.float32)
            south = fourier_ref[1, k, rows, :].astype(jnp.float32)
            out_ref[q, 0, k] = jnp.where(keep, north + south, 0.0).astype(out_ref.dtype)
            out_ref[q, 1, k] = jnp.where(keep, north - south, 0.0).astype(out_ref.dtype)


def make_parts(fourier, cycle_points, wave_table, groups):
    _, cycles, waves, channels = fourier.shape
    width = waves // groups
    return pl.pallas_call(
        functools.partial(parts_kernel, groups, width),
        out_shape=jax.ShapeDtypeStruct((groups, 2, cycles, width, channels), fourier.dtype),
        in_specs=[
            pl.BlockSpec(memory_space=pltpu.SMEM),
            pl.BlockSpec(memory_space=pltpu.SMEM),
            pl.BlockSpec(memory_space=pltpu.VMEM),
        ],
        out_specs=pl.BlockSpec(memory_space=pltpu.VMEM),
        name="make_parts",
    )(cycle_points, wave_table, fourier)


def band_kernel(me_ref, parts_ref, legendre_ref, *refs):
    mine_ref, near_ref, far_ref, cross_ref = refs[-4:]
    me = me_ref[0]
    cols = mine_ref.shape[1]
    for slot in range(mine_ref.shape[0]):
        for flip, ref in ((3, cross_ref), (2, far_ref), (0, mine_ref), (1, near_ref)):
            shard = me ^ flip
            piece = legendre_ref[slot, :, pl.ds(pl.multiple_of(shard * cols, cols), cols)]
            total = lax.dot_general(
                piece, parts_ref[shard // 2, slot], (((0,), (0,)), ((), ())), preferred_element_type=jnp.float32
            )
            ref[slot] = total.astype(ref.dtype)


def band_sums(me, parts, legendre, first, whole):
    _, slots, cycles, channels = parts.shape
    columns = legendre.shape[2]
    cols = columns // 4
    step = 2 if slots % 2 == 0 else 1
    skip = first // step
    every = jax.ShapeDtypeStruct((legendre.shape[0], cols, channels), parts.dtype)
    chunk = jax.ShapeDtypeStruct((slots, cols, channels), parts.dtype)
    every_spec = pl.BlockSpec((step, cols, channels), lambda m, w: (skip + m, 0, 0))
    chunk_spec = pl.BlockSpec((step, cols, channels), lambda m, w: (m, 0, 0))
    return pl.pallas_call(
        band_kernel,
        grid_spec=pltpu.PrefetchScalarGridSpec(
            num_scalar_prefetch=1,
            grid=(slots // step,),
            in_specs=[
                pl.BlockSpec((2, step, cycles, channels), lambda m, w: (0, m, 0, 0)),
                pl.BlockSpec((step, cycles, columns), lambda m, w: (skip + m, 0, 0)),
            ]
            + [pl.BlockSpec(memory_space=pl.ANY)] * len(whole),
            out_specs=[every_spec, chunk_spec, chunk_spec, chunk_spec],
        ),
        out_shape=[every, chunk, chunk, chunk],
        input_output_aliases={3 + i: i for i in range(len(whole))},
        name="band_sums",
        cost_estimate=pl.CostEstimate(
            flops=2 * slots * cycles * channels * columns,
            bytes_accessed=slots * cycles * columns * 2,
            transcendentals=0,
        ),
    )(me, parts, legendre, *whole)


def final_kernel(mine_ref, near_ref, end_ref, *refs):
    total = mine_ref[...].astype(jnp.float32) + near_ref[...].astype(jnp.float32)
    refs[-1][...] = (total + end_ref[...].astype(jnp.float32)).astype(refs[-1].dtype)


def finish(mine, near, end, first, whole):
    slots, cols, channels = end.shape
    step = 2 if slots % 2 == 0 else 1
    skip = first // step
    every_spec = pl.BlockSpec((step, cols, channels), lambda m: (skip + m, 0, 0))
    chunk_spec = pl.BlockSpec((step, cols, channels), lambda m: (m, 0, 0))
    return pl.pallas_call(
        final_kernel,
        grid=(slots // step,),
        in_specs=[every_spec, chunk_spec, chunk_spec] + [pl.BlockSpec(memory_space=pl.ANY)] * len(whole),
        out_specs=every_spec,
        out_shape=jax.ShapeDtypeStruct(mine.shape, mine.dtype),
        input_output_aliases={3: 0} if whole else {},
        name="finish",
        cost_estimate=pl.CostEstimate(flops=0, bytes_accessed=FINISH_BYTES * slots, transcendentals=0),
    )(mine, near, end, *whole)


def after(value, *earlier):
    return lax.optimization_barrier((value, *earlier))[0]


def add(*values):
    return sum(v.astype(jnp.float32) for v in values).astype(jnp.bfloat16)


def per_device(fourier, cycle_points, wave_table, legendre):
    groups = lax.axis_size("wave")
    me = lax.axis_index("lat")[None]
    sent = make_parts(fourier, cycle_points, wave_table, groups)
    got = lax.all_to_all(sent, "wave", split_axis=0, concat_axis=0, tiled=True)
    _, _, cycles, width, channels = got.shape
    one = [(i, i ^ 1) for i in range(4)]
    two = [(i, i ^ 2) for i in range(4)]
    mine = ()
    crosses, nears, fars = [], [], []
    first = 0
    for size in CHUNKS:
        rows = lax.slice_in_dim(got, first, first + size, axis=3)
        parts = jnp.transpose(rows, (1, 3, 0, 2, 4)).reshape(2, size, groups * cycles, channels)
        whole, near, far, cross = band_sums(me, parts, legendre, first, mine)
        mine = (whole,)
        got = after(got, far)
        crosses.append(lax.ppermute(cross, "lat", one))
        nears.append(near)
        fars.append(far)
        first += size
    (mine,) = mine
    pair = mine
    ends = []
    for i, (far, cross) in enumerate(zip(fars, crosses)):
        pair = add(far, after(cross, pair))
        ends.append(lax.ppermute(pair, "lat", two))
        if LATE:
            nears[i] = after(nears[i], pair)
    out = ()
    first = 0
    for size, near, end in zip(CHUNKS, nears, ends):
        out = (finish(mine, lax.ppermute(near, "lat", one), end, first, out),)
        first += size
    return out[0]


def solution(mesh):
    placed = (P(None, ("lat", "wave"), None, None), P(("lat", "wave")), P(), P("wave", "lat", None))
    return jax.shard_map(
        per_device, mesh=mesh, in_specs=placed, out_specs=P("wave", "lat", None), check_vma=False
    )
```

time: 192 us -> 154 us (0.80)
  blocking collectives: 167 us -> 0 us
  waiting for transfers between devices: 0 us -> 78.6 us
  starting transfers between devices: 0 us -> 41.7 us
  Pallas kernels: 17.8 us -> 24.8 us
  local copies, waits for them, and re-layouts: 3.77 us -> 8.53 us
  other arithmetic: 3.08 us -> 0.29 us
    all_to_all x2 -> x0, blocking collectives: 167 us -> none  [the longest x1 114 us: per_device(): moved = lax.all_to_all(sums, 'lat', split_axis=0, concat_axis=0, tiled=True)]
    ppermute x0 -> x12, waiting for transfers between devices: none -> 40.8 us  [the longest x4 22.4 us: per_device(): out = (finish(mine, lax.ppermute(near, 'lat', one), end, first, out),)]
    all_to_all x0 -> x1, waiting for transfers between devices: none -> 37.8 us  [per_device(): got = lax.all_to_all(sent, 'wave', split_axis=0, concat_axis=0, tiled=True)]
    ppermute x0 -> x12, starting transfers between devices: none -> 26.1 us  [the longest x4 18.4 us: per_device(): crosses.append(lax.ppermute(cross, 'lat', one))]
    all_to_all x0 -> x1, starting transfers between devices: none -> 15.6 us  [per_device(): got = lax.all_to_all(sent, 'wave', split_axis=0, concat_axis=0, tiled=True)]
    pallas_call x1 -> x8, Pallas kernels: 13.3 us -> 20.3 us  [the longest x4 12.7 us: band_sums(): pl.pallas_call(band_kernel, grid_spec=pltpu.PrefetchScalarGridSpec(num_sc...]
    unnamed x0 -> x28, local copies, waits for them, and re-layouts: none -> 3.55 us
    reduce_sum x1 -> x0, other arithmetic: 3.08 us -> none  [per_device(): total = jnp.sum(moved.astype(jnp.float32), axis=0).astype(jnp.bfloat16)]
  transfers between devices with their start and end apart: 0 -> 13, of which waited for: 0 -> 6; matrix products, arithmetic and copies ran while one was open for 0% -> 3% of each run, Pallas kernels for 0% -> 10%
where the time goes in v2:
time: 154 us
  waiting for transfers between devices  78.6 us (51%)
  starting transfers between devices  41.7 us (27%)
  Pallas kernels  24.8 us (16%)
  local copies, waits for them, and re-layouts  8.53 us (6%)
    all_to_all x1, waiting for transfers between devices, per_device(): got = lax.all_to_all(sent, 'wave', split_axis=0, concat_axis=0, tiled=True)  37.8 us
    ppermute x4, waiting for transfers between devices, per_device(): out = (finish(mine, lax.ppermute(near, 'lat', one), end, first, out),)  22.4 us
    ppermute x4, waiting for transfers between devices, per_device(): crosses.append(lax.ppermute(cross, 'lat', one))  18.4 us
    ppermute x4, starting transfers between devices, per_device(): crosses.append(lax.ppermute(cross, 'lat', one))  18.4 us
    all_to_all x1, starting transfers between devices, per_device(): got = lax.all_to_all(sent, 'wave', split_axis=0, concat_axis=0, tiled=True)  15.6 us
    pallas_call x4, Pallas kernels, band_sums(): pl.pallas_call(band_kernel, grid_spec=pltpu.PrefetchScalarGridSpec(num_sc...  12.7 us
    pallas_call x4, Pallas kernels, finish(): pl.pallas_call(final_kernel, grid=(slots // step,), in_specs=[every_spec,...  7.64 us
    ppermute x4, starting transfers between devices, per_device(): ends.append(lax.ppermute(pair, 'lat', two))  6.33 us
  transfers between devices with their start and end apart: 13, of which 6 were waited for; matrix products, arithmetic and copies ran while one was open for 3% of the time, Pallas kernels for 10%

profile of v2, /device:TPU:1, one launch (start us, length us, event | category | flops | bytes accessed | tf_op | source)
XLA Modules:
  0.0 154.1 jit_solution(16694601987488415809)
XLA Ops:
  0.0 4.4 %make_parts.1 = bf16[64,2,4,16,128]{4,3,2,1,0:T(8,128)(2,1)} custom-call(s32[4]{0:T(128)} %points_ref.1, s32[1024]{0:T(1024)} %table_ref.1, bf16[2,4,1024,128]{3,2,1,0:T(8,128)(2,1)} %fourier_ref.1), custom_call_target="tpu_custom_call" | custom-call | tf_op jit(solution)/shard_map/make_parts/pallas_call | solution.py:35
  4.4 15.6 %all-to-all-start = ((bf16[64,2,4,16,128]{4,3,2,1,0:T(8,128)(2,1)}), bf16[64,2,4,16,128]{4,3,2,1,0:T(8,128)(2,1)S(1)}, u32[]{:S(2)}, u32[]{:S(2)}) async-start(bf16[64,2,4,16,128]{4,3,2,1,0:T(8,128)(2,1)} %make_parts.1), calls=%async_computation | async-start | bytes 4194304 | tf_op jit(solution)/shard_map/all_to_all | solution.py:130
  20.1 37.8 %all-to-all-done = bf16[64,2,4,16,128]{4,3,2,1,0:T(8,128)(2,1)S(1)} async-done(((bf16[64,2,4,16,128]{4,3,2,1,0:T(8,128)(2,1)}), bf16[64,2,4,16,128]{4,3,2,1,0:T(8,128)(2,1)S(1)}, u32[]{:S(2)}, u32[]{:S(2)}) %all-to-all-start) | async-done | bytes 2097184 | tf_op jit(solution)/shard_map/all_to_all | solution.py:130
  57.9 0.2 slice_bitcast_fusion
  58.1 1.0 copy.11
  59.1 3.1 %band_sums.4 = (bf16[16,256,128]{2,1,0:T(8,128)(2,1)}, bf16[4,256,128]{2,1,0:T(8,128)(2,1)}, bf16[4,256,128]{2,1,0:T(8,128)(2,1)}, bf16[4,256,128]{2,1,0:T(8,128)(2,1)}) custom-call(s32[1]{0:T(128)} %bitcast.me_ref, bf16[2,4,256,128]{3,2,1,0:T(8,128)(2,1)} %bitcast.16, bf16[16,256,1024]{2,1,0:T(8,128)(2,1)} %legendre_ref.7), custom_call_target="tpu_custom_call" | custom-call | flops 268435456 | bytes 2097152 | tf_op jit(solution)/shard_map/band_sums/pallas_call | solution.py:72
  62.3 16.7 %collective-permute-start.3 = (bf16[4,256,128]{2,1,0:T(8,128)(2,1)}, bf16[4,256,128]{2,1,0:T(8,128)(2,1)S(1)}, u32[]{:S(2)}, u32[]{:S(2)}) collective-permute-start(bf16[4,256,128]{2,1,0:T(8,128)(2,1)} %get-tuple-element.47), channel_id=1, source_target_pairs={{0,64},{64,0},{128,192},{192,128},{1,65},{65,1},{129,193},{193,129... | collective-permute-start | bytes 786440 | tf_op jit(solution)/shard_map/ppermute | solution.py:143
  79.0 0.3 slice_bitcast_fusion.3
  79.2 1.0 copy.12
  80.2 3.2 %band_sums.5 = (bf16[16,256,128]{2,1,0:T(8,128)(2,1)}, bf16[4,256,128]{2,1,0:T(8,128)(2,1)}, bf16[4,256,128]{2,1,0:T(8,128)(2,1)}, bf16[4,256,128]{2,1,0:T(8,128)(2,1)}) custom-call(s32[1]{0:T(128)} %bitcast.me_ref, bf16[2,4,256,128]{3,2,1,0:T(8,128)(2,1)} %bitcast.14, bf16[16,256,1024]{2,1,0:T(8,128)(2,1)} %legendre_ref.7, ...), custom_call_target="tpu_custom_call", output_to_operand_aliasing={{0}: (3, {})} | custom-call | flops 268435456 | bytes 2097152 | tf_op jit(solution)/shard_map/band_sums/pallas_call | solution.py:72
  83.4 0.0 collective-permute-start.2
  83.4 0.2 slice_bitcast_fusion.2
  83.7 1.0 copy.13
  84.7 3.1 %band_sums.6 = (bf16[16,256,128]{2,1,0:T(8,128)(2,1)}, bf16[4,256,128]{2,1,0:T(8,128)(2,1)}, bf16[4,256,128]{2,1,0:T(8,128)(2,1)}, bf16[4,256,128]{2,1,0:T(8,128)(2,1)}) custom-call(s32[1]{0:T(128)} %bitcast.me_ref, bf16[2,4,256,128]{3,2,1,0:T(8,128)(2,1)} %bitcast.15, bf16[16,256,1024]{2,1,0:T(8,128)(2,1)} %legendre_ref.7, ...), custom_call_target="tpu_custom_call", output_to_operand_aliasing={{0}: (3, {})} | custom-call | flops 268435456 | bytes 2097152 | tf_op jit(solution)/shard_map/band_sums/pallas_call | solution.py:72
  87.8 0.3 slice_bitcast_fusion.1
  88.1 1.0 copy.14
  89.1 0.0 copy-start.13
  89.1 3.3 %band_sums.7 = (bf16[16,256,128]{2,1,0:T(8,128)(2,1)}, bf16[4,256,128]{2,1,0:T(8,128)(2,1)}, bf16[4,256,128]{2,1,0:T(8,128)(2,1)}, bf16[4,256,128]{2,1,0:T(8,128)(2,1)}) custom-call(s32[1]{0:T(128)} %bitcast.me_ref, bf16[2,4,256,128]{3,2,1,0:T(8,128)(2,1)} %bitcast.13, bf16[16,256,1024]{2,1,0:T(8,128)(2,1)} %legendre_ref.7, ...), custom_call_target="tpu_custom_call", output_to_operand_aliasing={{0}: (3, {})} | custom-call | flops 268435456 | bytes 2097152 | tf_op jit(solution)/shard_map/band_sums/pallas_call | solution.py:72
  92.4 1.5 %collective-permute-start = (bf16[4,256,128]{2,1,0:T(8,128)(2,1)}, bf16[4,256,128]{2,1,0:T(8,128)(2,1)S(1)}, u32[]{:S(2)}, u32[]{:S(2)}) collective-permute-start(bf16[4,256,128]{2,1,0:T(8,128)(2,1)} %get-tuple-element.44), channel_id=1, source_target_pairs={{0,64},{64,0},{128,192},{192,128},{1,65},{65,1},{129,193},{193,129... | collective-permute-start | bytes 786440 | tf_op jit(solution)/shard_map/ppermute | solution.py:143
  93.9 0.0 copy-done.13
  93.9 0.1 collective-permute-start.1
  94.0 0.0 collective-permute-done.3
  94.0 0.0 copy-done.9
  94.0 0.1 add_convert_fusion.3
  94.1 2.1 %collective-permute-start.11 = (bf16[4,256,128]{2,1,0:T(8,128)(2,1)S(1)}, bf16[4,256,128]{2,1,0:T(8,128)(2,1)S(1)}, u32[]{:S(2)}, u32[]{:S(2)}) collective-permute-start(bf16[4,256,128]{2,1,0:T(8,128)(2,1)S(1)} %add_convert_fusion.3), channel_id=1, source_target_pairs={{0,128},{64,192},{128,0},{192,64},{1,129},{65,193},{129,1},{193,65... | collective-permute-start | bytes 786440 | tf_op jit(solution)/shard_map/ppermute | solution.py:152
  96.2 0.0 collective-permute-done.2
  96.2 0.0 copy-done.10
  96.2 0.1 add_convert_fusion.2
  96.3 0.5 collective-permute-start.9
  96.7 1.4 collective-permute-start.8
  98.1 18.4 %collective-permute-done.1 = bf16[4,256,128]{2,1,0:T(8,128)(2,1)S(1)} collective-permute-done((bf16[4,256,128]{2,1,0:T(8,128)(2,1)S(1)}, bf16[4,256,128]{2,1,0:T(8,128)(2,1)S(1)}, u32[]{:S(2)}, u32[]{:S(2)}) %collective-permute-start.1) | collective-permute-done | bytes 262176 | tf_op jit(solution)/shard_map/ppermute | solution.py:143
  116.5 0.0 collective-permute-start.10
  116.5 0.0 copy-done.8
  116.5 0.1 add_convert_fusion.1
  116.6 0.0 collective-permute-done
  116.6 1.8 %collective-permute-start.7 = (bf16[4,256,128]{2,1,0:T(8,128)(2,1)S(1)}, bf16[4,256,128]{2,1,0:T(8,128)(2,1)S(1)}, u32[]{:S(2)}, u32[]{:S(2)}) collective-permute-start(bf16[4,256,128]{2,1,0:T(8,128)(2,1)S(1)} %add_convert_fusion.1), channel_id=1, source_target_pairs={{0,128},{64,192},{128,0},{192,64},{1,129},{65,193},{129,1},{193,65... | collective-permute-start | bytes 786440 | tf_op jit(solution)/shard_map/ppermute | solution.py:152
  118.3 0.0 copy-done.7
  118.3 0.1 add_convert_fusion
  118.4 9.9 %collective-permute-done.8.near_ref = bf16[4,256,128]{2,1,0:T(8,128)(2,1)S(1)} collective-permute-done((bf16[4,256,128]{2,1,0:T(8,128)(2,1)}, bf16[4,256,128]{2,1,0:T(8,128)(2,1)S(1)}, u32[]{:S(2)}, u32[]{:S(2)}) %collective-permute-start.8) | collective-permute-done | bytes 262176 | tf_op jit(solution)/shard_map/ppermute | solution.py:158
  128.3 0.0 collective-permute-start.6
  128.3 5.6 %collective-permute-done.10.near_ref = bf16[4,256,128]{2,1,0:T(8,128)(2,1)S(1)} collective-permute-done((bf16[4,256,128]{2,1,0:T(8,128)(2,1)}, bf16[4,256,128]{2,1,0:T(8,128)(2,1)S(1)}, u32[]{:S(2)}, u32[]{:S(2)}) %collective-permute-start.10) | collective-permute-done | bytes 262176 | tf_op jit(solution)/shard_map/ppermute | solution.py:158
  133.9 0.0 copy-done.12
  133.9 0.0 collective-permute-start.4
  133.9 0.0 collective-permute-done.11.end_ref
  133.9 0.0 copy-start.6
  133.9 2.0 %collective-permute-start.5 = (bf16[4,256,128]{2,1,0:T(8,128)(2,1)S(1)}, bf16[4,256,128]{2,1,0:T(8,128)(2,1)S(1)}, u32[]{:S(2)}, u32[]{:S(2)}) collective-permute-start(bf16[4,256,128]{2,1,0:T(8,128)(2,1)S(1)} %add_convert_fusion), channel_id=1, source_target_pairs={{0,128},{64,192},{128,0},{192,64},{1,129},{65,193},{129,1},{193,65... | collective-permute-start | bytes 786440 | tf_op jit(solution)/shard_map/ppermute | solution.py:152
  136.0 0.0 copy-done.11
  136.0 0.0 copy-done.6
  136.0 1.9 %finish.4.refs_0_ = bf16[16,256,128]{2,1,0:T(8,128)(2,1)} custom-call(bf16[16,256,128]{2,1,0:T(8,128)(2,1)} %get-tuple-element.41.mine_ref, bf16[4,256,128]{2,1,0:T(8,128)(2,1)} %copy-done.11, bf16[4,256,128]{2,1,0:T(8,128)(2,1)} %copy-done.6), custom_call_target="tpu_custom_call" | custom-call | bytes 32000000 | tf_op jit(solution)/shard_map/finish/pallas_call | solution.py:106
  137.9 0.0 collective-permute-done.9.end_ref
  137.9 0.0 copy-done.1
  137.9 0.0 copy-start
  137.9 0.7 copy-done
  138.6 1.9 %finish.5.refs_0_ = bf16[16,256,128]{2,1,0:T(8,128)(2,1)} custom-call(bf16[16,256,128]{2,1,0:T(8,128)(2,1)} %get-tuple-element.41.mine_ref, bf16[4,256,128]{2,1,0:T(8,128)(2,1)} %copy-done.1, bf16[4,256,128]{2,1,0:T(8,128)(2,1)} %copy-done, bf16[16,256,128]{2,1,0:T(8,128)(2,1)} %finish.4.refs_0_), custom_call_target="tpu_custom_call", output_to_operand_aliasing={{}: (3, {})} | custom-call | bytes 32000000 | tf_op jit(solution)/shard_map/finish/pallas_call | solution.py:106
  140.5 4.6 %collective-permute-done.6.near_ref = bf16[4,256,128]{2,1,0:T(8,128)(2,1)S(1)} collective-permute-done((bf16[4,256,128]{2,1,0:T(8,128)(2,1)}, bf16[4,256,128]{2,1,0:T(8,128)(2,1)S(1)}, u32[]{:S(2)}, u32[]{:S(2)}) %collective-permute-start.6) | collective-permute-done | bytes 262176 | tf_op jit(solution)/shard_map/ppermute | solution.py:158
  145.1 0.0 collective-permute-done.7.end_ref
  145.1 0.7 copy-done.4
  145.8 0.7 copy-done.2
  146.5 1.9 %finish.6.refs_0_ = bf16[16,256,128]{2,1,0:T(8,128)(2,1)} custom-call(bf16[16,256,128]{2,1,0:T(8,128)(2,1)} %get-tuple-element.41.mine_ref, bf16[4,256,128]{2,1,0:T(8,128)(2,1)} %copy-done.4, bf16[4,256,128]{2,1,0:T(8,128)(2,1)} %copy-done.2, bf16[16,256,128]{2,1,0:T(8,128)(2,1)} %finish.5.refs_0_), custom_call_target="tpu_custom_call", output_to_operand_aliasing={{}: (3, {})} | custom-call | bytes 32000000 | tf_op jit(solution)/shard_map/finish/pallas_call | solution.py:106
  148.5 2.3 %collective-permute-done.4.near_ref = bf16[4,256,128]{2,1,0:T(8,128)(2,1)S(1)} collective-permute-done((bf16[4,256,128]{2,1,0:T(8,128)(2,1)S(1)}, bf16[4,256,128]{2,1,0:T(8,128)(2,1)S(1)}, u32[]{:S(2)}, u32[]{:S(2)}) %collective-permute-start.4) | collective-permute-done | bytes 262176 | tf_op jit(solution)/shard_map/ppermute | solution.py:158
  150.8 0.0 collective-permute-done.5.end_ref
  150.8 0.7 copy-done.3
  151.5 0.7 copy-done.5
  152.2 1.9 %finish.7 = bf16[16,256,128]{2,1,0:T(8,128)(2,1)} custom-call(bf16[16,256,128]{2,1,0:T(8,128)(2,1)} %get-tuple-element.41.mine_ref, bf16[4,256,128]{2,1,0:T(8,128)(2,1)} %copy-done.3, bf16[4,256,128]{2,1,0:T(8,128)(2,1)} %copy-done.5, bf16[16,256,128]{2,1,0:T(8,128)(2,1)} %finish.6.refs_0_), custom_call_target="tpu_custom_call", output_to_operand_aliasing={{}: (3, {})} | custom-call | bytes 32000000 | tf_op jit(solution)/shard_map/finish/pallas_call | solution.py:106
  (11 shorter events, 0.0 us)
Async XLA Ops:
  4.4 53.4 %all-to-all-start = ((bf16[64,2,4,16,128]{4,3,2,1,0:T(8,128)(2,1)}), bf16[64,2,4,16,128]{4,3,2,1,0:T(8,128)(2,1)S(1)}, u32[]{:S(2)}, u32[]{:S(2)}) async-start(bf16[64,2,4,16,128]{4,3,2,1,0:T(8,128)(2,1)} %make_parts.1), calls=%async_computation | async-start | bytes 4194304 | tf_op jit(solution)/shard_map/all_to_all | solution.py:130
  62.3 31.8 %collective-permute-start.3 = (bf16[4,256,128]{2,1,0:T(8,128)(2,1)}, bf16[4,256,128]{2,1,0:T(8,128)(2,1)S(1)}, u32[]{:S(2)}, u32[]{:S(2)}) collective-permute-start(bf16[4,256,128]{2,1,0:T(8,128)(2,1)} %get-tuple-element.47), channel_id=1, source_target_pairs={{0,64},{64,0},{128,192},{192,128},{1,65},{65,1},{129,193},{193,129... | collective-permute-start | bytes 786440 | tf_op jit(solution)/shard_map/ppermute | solution.py:143
  83.4 12.8 %collective-permute-start.2 = (bf16[4,256,128]{2,1,0:T(8,128)(2,1)}, bf16[4,256,128]{2,1,0:T(8,128)(2,1)S(1)}, u32[]{:S(2)}, u32[]{:S(2)}) collective-permute-start(bf16[4,256,128]{2,1,0:T(8,128)(2,1)} %get-tuple-element.46), channel_id=1, source_target_pairs={{0,64},{64,0},{128,192},{192,128},{1,65},{65,1},{129,193},{193,129... | collective-permute-start | bytes 786440 | tf_op jit(solution)/shard_map/ppermute | solution.py:143
  89.1 4.8 %copy-start.13 = (bf16[4,256,128]{2,1,0:T(8,128)(2,1)S(1)}, bf16[4,256,128]{2,1,0:T(8,128)(2,1)}, u32[]{:S(2)}) copy-start(bf16[4,256,128]{2,1,0:T(8,128)(2,1)} %get-tuple-element.45) | copy-start | bytes 786436
  89.1 4.9 %copy-start.9 = (bf16[4,256,128]{2,1,0:T(8,128)(2,1)S(1)}, bf16[4,256,128]{2,1,0:T(8,128)(2,1)}, u32[]{:S(2)}) copy-start(bf16[4,256,128]{2,1,0:T(8,128)(2,1)} %get-tuple-element.32) | copy-start | bytes 786436
  89.1 7.1 %copy-start.10 = (bf16[4,256,128]{2,1,0:T(8,128)(2,1)S(1)}, bf16[4,256,128]{2,1,0:T(8,128)(2,1)}, u32[]{:S(2)}) copy-start(bf16[4,256,128]{2,1,0:T(8,128)(2,1)} %get-tuple-element.35) | copy-start | bytes 786436
  89.1 27.4 %copy-start.8 = (bf16[4,256,128]{2,1,0:T(8,128)(2,1)S(1)}, bf16[4,256,128]{2,1,0:T(8,128)(2,1)}, u32[]{:S(2)}) copy-start(bf16[4,256,128]{2,1,0:T(8,128)(2,1)} %get-tuple-element.38) | copy-start | bytes 786436
  92.4 26.0 %copy-start.7 = (bf16[4,256,128]{2,1,0:T(8,128)(2,1)S(1)}, bf16[4,256,128]{2,1,0:T(8,128)(2,1)}, u32[]{:S(2)}) copy-start(bf16[4,256,128]{2,1,0:T(8,128)(2,1)} %get-tuple-element.43) | copy-start | bytes 786436
  92.4 41.5 %copy-start.12 = (bf16[4,256,128]{2,1,0:T(8,128)(2,1)S(1)}, bf16[4,256,128]{2,1,0:T(8,128)(2,1)}, u32[]{:S(2)}) copy-start(bf16[4,256,128]{2,1,0:T(8,128)(2,1)} %get-tuple-element.52) | copy-start | bytes 786436
  92.4 24.2 %collective-permute-start = (bf16[4,256,128]{2,1,0:T(8,128)(2,1)}, bf16[4,256,128]{2,1,0:T(8,128)(2,1)S(1)}, u32[]{:S(2)}, u32[]{:S(2)}) collective-permute-start(bf16[4,256,128]{2,1,0:T(8,128)(2,1)} %get-tuple-element.44), channel_id=1, source_target_pairs={{0,64},{64,0},{128,192},{192,128},{1,65},{65,1},{129,193},{193,129... | collective-permute-start | bytes 786440 | tf_op jit(solution)/shard_map/ppermute | solution.py:143
  93.9 22.6 %collective-permute-start.1 = (bf16[4,256,128]{2,1,0:T(8,128)(2,1)S(1)}, bf16[4,256,128]{2,1,0:T(8,128)(2,1)S(1)}, u32[]{:S(2)}, u32[]{:S(2)}) collective-permute-start(bf16[4,256,128]{2,1,0:T(8,128)(2,1)S(1)} %copy-done.13), channel_id=1, source_target_pairs={{0,64},{64,0},{128,192},{192,128},{1,65},{65,1},{129,193},{193,129... | collective-permute-start | bytes 786440 | tf_op jit(solution)/shard_map/ppermute | solution.py:143
  94.1 39.8 %collective-permute-start.11 = (bf16[4,256,128]{2,1,0:T(8,128)(2,1)S(1)}, bf16[4,256,128]{2,1,0:T(8,128)(2,1)S(1)}, u32[]{:S(2)}, u32[]{:S(2)}) collective-permute-start(bf16[4,256,128]{2,1,0:T(8,128)(2,1)S(1)} %add_convert_fusion.3), channel_id=1, source_target_pairs={{0,128},{64,192},{128,0},{192,64},{1,129},{65,193},{129,1},{193,65... | collective-permute-start | bytes 786440 | tf_op jit(solution)/shard_map/ppermute | solution.py:152
  96.3 41.6 %collective-permute-start.9 = (bf16[4,256,128]{2,1,0:T(8,128)(2,1)S(1)}, bf16[4,256,128]{2,1,0:T(8,128)(2,1)S(1)}, u32[]{:S(2)}, u32[]{:S(2)}) collective-permute-start(bf16[4,256,128]{2,1,0:T(8,128)(2,1)S(1)} %add_convert_fusion.2), channel_id=1, source_target_pairs={{0,128},{64,192},{128,0},{192,64},{1,129},{65,193},{129,1},{193,65... | collective-permute-start | bytes 786440 | tf_op jit(solution)/shard_map/ppermute | solution.py:152
  96.7 31.6 %collective-permute-start.8 = (bf16[4,256,128]{2,1,0:T(8,128)(2,1)}, bf16[4,256,128]{2,1,0:T(8,128)(2,1)S(1)}, u32[]{:S(2)}, u32[]{:S(2)}) collective-permute-start(bf16[4,256,128]{2,1,0:T(8,128)(2,1)} %get-tuple-element.56), channel_id=1, source_target_pairs={{0,64},{64,0},{128,192},{192,128},{1,65},{65,1},{129,193},{193,129... | collective-permute-start | bytes 786440 | tf_op jit(solution)/shard_map/ppermute | solution.py:158
  116.5 17.4 %collective-permute-start.10 = (bf16[4,256,128]{2,1,0:T(8,128)(2,1)}, bf16[4,256,128]{2,1,0:T(8,128)(2,1)S(1)}, u32[]{:S(2)}, u32[]{:S(2)}) collective-permute-start(bf16[4,256,128]{2,1,0:T(8,128)(2,1)} %get-tuple-element.58), channel_id=1, source_target_pairs={{0,64},{64,0},{128,192},{192,128},{1,65},{65,1},{129,193},{193,129... | collective-permute-start | bytes 786440 | tf_op jit(solution)/shard_map/ppermute | solution.py:158
  116.6 28.6 %collective-permute-start.7 = (bf16[4,256,128]{2,1,0:T(8,128)(2,1)S(1)}, bf16[4,256,128]{2,1,0:T(8,128)(2,1)S(1)}, u32[]{:S(2)}, u32[]{:S(2)}) collective-permute-start(bf16[4,256,128]{2,1,0:T(8,128)(2,1)S(1)} %add_convert_fusion.1), channel_id=1, source_target_pairs={{0,128},{64,192},{128,0},{192,64},{1,129},{65,193},{129,1},{193,65... | collective-permute-start | bytes 786440 | tf_op jit(solution)/shard_map/ppermute | solution.py:152
  128.3 9.6 %copy-start.1 = (bf16[4,256,128]{2,1,0:T(8,128)(2,1)}, bf16[4,256,128]{2,1,0:T(8,128)(2,1)S(1)}, u32[]{:S(2)}) copy-start(bf16[4,256,128]{2,1,0:T(8,128)(2,1)S(1)} %collective-permute-done.8.near_ref) | copy-start | bytes 786436
  128.3 16.9 %collective-permute-start.6 = (bf16[4,256,128]{2,1,0:T(8,128)(2,1)}, bf16[4,256,128]{2,1,0:T(8,128)(2,1)S(1)}, u32[]{:S(2)}, u32[]{:S(2)}) collective-permute-start(bf16[4,256,128]{2,1,0:T(8,128)(2,1)} %get-tuple-element.54), channel_id=1, source_target_pairs={{0,64},{64,0},{128,192},{192,128},{1,65},{65,1},{129,193},{193,129... | collective-permute-start | bytes 786440 | tf_op jit(solution)/shard_map/ppermute | solution.py:158
  133.9 2.1 %copy-start.11 = (bf16[4,256,128]{2,1,0:T(8,128)(2,1)}, bf16[4,256,128]{2,1,0:T(8,128)(2,1)S(1)}, u32[]{:S(2)}) copy-start(bf16[4,256,128]{2,1,0:T(8,128)(2,1)S(1)} %collective-permute-done.10.near_ref) | copy-start | bytes 786436
  133.9 16.8 %collective-permute-start.4 = (bf16[4,256,128]{2,1,0:T(8,128)(2,1)S(1)}, bf16[4,256,128]{2,1,0:T(8,128)(2,1)S(1)}, u32[]{:S(2)}, u32[]{:S(2)}) collective-permute-start(bf16[4,256,128]{2,1,0:T(8,128)(2,1)S(1)} %copy-done.12), channel_id=1, source_target_pairs={{0,64},{64,0},{128,192},{192,128},{1,65},{65,1},{129,193},{193,129... | collective-permute-start | bytes 786440 | tf_op jit(solution)/shard_map/ppermute | solution.py:158
  133.9 2.0 %copy-start.6 = (bf16[4,256,128]{2,1,0:T(8,128)(2,1)}, bf16[4,256,128]{2,1,0:T(8,128)(2,1)S(1)}, u32[]{:S(2)}) copy-start(bf16[4,256,128]{2,1,0:T(8,128)(2,1)S(1)} %collective-permute-done.11.end_ref) | copy-start | bytes 786436
  133.9 16.8 %collective-permute-start.5 = (bf16[4,256,128]{2,1,0:T(8,128)(2,1)S(1)}, bf16[4,256,128]{2,1,0:T(8,128)(2,1)S(1)}, u32[]{:S(2)}, u32[]{:S(2)}) collective-permute-start(bf16[4,256,128]{2,1,0:T(8,128)(2,1)S(1)} %add_convert_fusion), channel_id=1, source_target_pairs={{0,128},{64,192},{128,0},{192,64},{1,129},{65,193},{129,1},{193,65... | collective-permute-start | bytes 786440 | tf_op jit(solution)/shard_map/ppermute | solution.py:152
  137.9 0.7 copy-start
  145.1 0.7 copy-start.4
  145.8 0.7 copy-start.2
  150.8 0.7 copy-start.3
  151.5 0.7 copy-start.5

commit v3 on v2

--- a/solution.py
+++ b/solution.py
@@ -9,7 +9,7 @@
 
 CHUNKS = (4,4,4,4)
 FINISH_BYTES = 8000000
-LATE = True
+LATE = 1
 
 
 def parts_kernel(groups, width, points_ref, table_ref, fourier_ref, out_ref):
@@ -146,12 +146,13 @@
         first += size
     (mine,) = mine
     pair = mine
-    ends = []
+    ends, pairs = [], []
     for i, (far, cross) in enumerate(zip(fars, crosses)):
-        pair = add(far, after(cross, pair))
+        held = [ends[-2]] if len(ends) >= 2 else []
+        pair = add(far, after(cross, pair, *held))
         ends.append(lax.ppermute(pair, "lat", two))
-        if LATE:
-            nears[i] = after(nears[i], pair)
+        pairs.append(pair)
+    nears = [after(near, pairs[min(i + LATE, len(pairs) - 1)]) for i, near in enumerate(nears)]
     out = ()
     first = 0
     for size, near, end in zip(CHUNKS, nears, ends):

time: 154 us -> 152 us (0.987); the launches traced: 154 us -> 149 us
  waiting for transfers between devices: 78.6 us -> 74.3 us
    ppermute x4, waiting for transfers between devices: 0.01 us -> 21.2 us  [per_device(): ends.append(lax.ppermute(pair, 'lat', two))]
    ppermute x4, waiting for transfers between devices: 18.4 us -> 0.01 us  [per_device(): crosses.append(lax.ppermute(cross, 'lat', one))]
    ppermute x4, waiting for transfers between devices: 22.4 us -> 15.2 us  [per_device(): out = (finish(mine, lax.ppermute(near, 'lat', one), end, first, out),)]
    ppermute x4, starting transfers between devices: 6.33 us -> 3.33 us  [per_device(): ends.append(lax.ppermute(pair, 'lat', two))]
    ppermute x4, starting transfers between devices: 1.37 us -> 3.09 us  [per_device(): out = (finish(mine, lax.ppermute(near, 'lat', one), end, first, out),)]
    unnamed x28 -> x30, local copies, waits for them, and re-layouts: 3.55 us -> 3.26 us
  transfers between devices with their start and end apart: 13 -> 13, of which waited for: 6 -> 7; matrix products, arithmetic and copies ran while one was open for 3% -> 3% of each run, Pallas kernels for 10% -> 10%
where the time goes in v3:
time: 152 us; the launch traced here: 149 us
  waiting for transfers between devices  74.3 us (49%)
  starting transfers between devices  41.7 us (27%)
  Pallas kernels  24.8 us (16%)
  local copies, waits for them, and re-layouts  8.23 us (5%)
    all_to_all x1, waiting for transfers between devices, per_device(): got = lax.all_to_all(sent, 'wave', split_axis=0, concat_axis=0, tiled=True)  37.8 us
    ppermute x4, waiting for transfers between devices, per_device(): ends.append(lax.ppermute(pair, 'lat', two))  21.2 us
    ppermute x4, starting transfers between devices, per_device(): crosses.append(lax.ppermute(cross, 'lat', one))  19.7 us
    all_to_all x1, starting transfers between devices, per_device(): got = lax.all_to_all(sent, 'wave', split_axis=0, concat_axis=0, tiled=True)  15.6 us
    ppermute x4, waiting for transfers between devices, per_device(): out = (finish(mine, lax.ppermute(near, 'lat', one), end, first, out),)  15.2 us
    pallas_call x4, Pallas kernels, band_sums(): pl.pallas_call(band_kernel, grid_spec=pltpu.PrefetchScalarGridSpec(num_sc...  12.7 us
    pallas_call x4, Pallas kernels, finish(): pl.pallas_call(final_kernel, grid=(slots // step,), in_specs=[every_spec,...  7.64 us
    transpose x8, local copies, waits for them, and re-layouts, per_device(): jnp.transpose(rows, (1, 3, 0, 2, 4))  4.98 us
  transfers between devices with their start and end apart: 13, of which 7 were waited for; matrix products, arithmetic and copies ran while one was open for 3% of the time, Pallas kernels for 10%

profile of v3, /device:TPU:1, one launch (start us, length us, event | category | flops | bytes accessed | tf_op | source)
XLA Modules:
  0.0 149.4 jit_solution(12791991433572769933)
XLA Ops:
  0.0 4.5 %make_parts.1 = bf16[64,2,4,16,128]{4,3,2,1,0:T(8,128)(2,1)} custom-call(s32[4]{0:T(128)} %points_ref.1, s32[1024]{0:T(1024)} %table_ref.1, bf16[2,4,1024,128]{3,2,1,0:T(8,128)(2,1)} %fourier_ref.1), custom_call_target="tpu_custom_call" | custom-call | tf_op jit(solution)/shard_map/make_parts/pallas_call | solution.py:35
  4.5 15.6 %all-to-all-start = ((bf16[64,2,4,16,128]{4,3,2,1,0:T(8,128)(2,1)}), bf16[64,2,4,16,128]{4,3,2,1,0:T(8,128)(2,1)S(1)}, u32[]{:S(2)}, u32[]{:S(2)}) async-start(bf16[64,2,4,16,128]{4,3,2,1,0:T(8,128)(2,1)} %make_parts.1), calls=%async_computation | async-start | bytes 4194304 | tf_op jit(solution)/shard_map/all_to_all | solution.py:130
  20.1 37.8 %all-to-all-done = bf16[64,2,4,16,128]{4,3,2,1,0:T(8,128)(2,1)S(1)} async-done(((bf16[64,2,4,16,128]{4,3,2,1,0:T(8,128)(2,1)}), bf16[64,2,4,16,128]{4,3,2,1,0:T(8,128)(2,1)S(1)}, u32[]{:S(2)}, u32[]{:S(2)}) %all-to-all-start) | async-done | bytes 2097184 | tf_op jit(solution)/shard_map/all_to_all | solution.py:130
  57.9 0.2 slice_bitcast_fusion
  58.1 1.0 copy.11
  59.1 3.1 %band_sums.4 = (bf16[16,256,128]{2,1,0:T(8,128)(2,1)}, bf16[4,256,128]{2,1,0:T(8,128)(2,1)}, bf16[4,256,128]{2,1,0:T(8,128)(2,1)}, bf16[4,256,128]{2,1,0:T(8,128)(2,1)}) custom-call(s32[1]{0:T(128)} %bitcast.me_ref, bf16[2,4,256,128]{3,2,1,0:T(8,128)(2,1)} %bitcast.16, bf16[16,256,1024]{2,1,0:T(8,128)(2,1)} %legendre_ref.7), custom_call_target="tpu_custom_call" | custom-call | flops 268435456 | bytes 2097152 | tf_op jit(solution)/shard_map/band_sums/pallas_call | solution.py:72
  62.3 16.7 %collective-permute-start.3 = (bf16[4,256,128]{2,1,0:T(8,128)(2,1)}, bf16[4,256,128]{2,1,0:T(8,128)(2,1)S(1)}, u32[]{:S(2)}, u32[]{:S(2)}) collective-permute-start(bf16[4,256,128]{2,1,0:T(8,128)(2,1)} %get-tuple-element.47), channel_id=1, source_target_pairs={{0,64},{64,0},{128,192},{192,128},{1,65},{65,1},{129,193},{193,129... | collective-permute-start | bytes 786440 | tf_op jit(solution)/shard_map/ppermute | solution.py:143
  79.0 0.3 slice_bitcast_fusion.3
  79.3 1.0 copy.12
  80.3 3.1 %band_sums.5 = (bf16[16,256,128]{2,1,0:T(8,128)(2,1)}, bf16[4,256,128]{2,1,0:T(8,128)(2,1)}, bf16[4,256,128]{2,1,0:T(8,128)(2,1)}, bf16[4,256,128]{2,1,0:T(8,128)(2,1)}) custom-call(s32[1]{0:T(128)} %bitcast.me_ref, bf16[2,4,256,128]{3,2,1,0:T(8,128)(2,1)} %bitcast.14, bf16[16,256,1024]{2,1,0:T(8,128)(2,1)} %legendre_ref.7, ...), custom_call_target="tpu_custom_call", output_to_operand_aliasing={{0}: (3, {})} | custom-call | flops 268435456 | bytes 2097152 | tf_op jit(solution)/shard_map/band_sums/pallas_call | solution.py:72
  83.4 0.0 collective-permute-start.2
  83.4 0.2 slice_bitcast_fusion.2
  83.6 1.0 copy.13
  84.6 3.1 %band_sums.6 = (bf16[16,256,128]{2,1,0:T(8,128)(2,1)}, bf16[4,256,128]{2,1,0:T(8,128)(2,1)}, bf16[4,256,128]{2,1,0:T(8,128)(2,1)}, bf16[4,256,128]{2,1,0:T(8,128)(2,1)}) custom-call(s32[1]{0:T(128)} %bitcast.me_ref, bf16[2,4,256,128]{3,2,1,0:T(8,128)(2,1)} %bitcast.15, bf16[16,256,1024]{2,1,0:T(8,128)(2,1)} %legendre_ref.7, ...), custom_call_target="tpu_custom_call", output_to_operand_aliasing={{0}: (3, {})} | custom-call | flops 268435456 | bytes 2097152 | tf_op jit(solution)/shard_map/band_sums/pallas_call | solution.py:72
  87.8 0.3 slice_bitcast_fusion.1
  88.1 1.0 copy.14
  89.1 1.5 collective-permute-start.1
  90.5 0.0 copy-start.10
  90.5 3.3 %band_sums.7 = (bf16[16,256,128]{2,1,0:T(8,128)(2,1)}, bf16[4,256,128]{2,1,0:T(8,128)(2,1)}, bf16[4,256,128]{2,1,0:T(8,128)(2,1)}, bf16[4,256,128]{2,1,0:T(8,128)(2,1)}) custom-call(s32[1]{0:T(128)} %bitcast.me_ref, bf16[2,4,256,128]{3,2,1,0:T(8,128)(2,1)} %bitcast.13, bf16[16,256,1024]{2,1,0:T(8,128)(2,1)} %legendre_ref.7, ...), custom_call_target="tpu_custom_call", output_to_operand_aliasing={{0}: (3, {})} | custom-call | flops 268435456 | bytes 2097152 | tf_op jit(solution)/shard_map/band_sums/pallas_call | solution.py:72
  93.8 0.0 copy-start.14
  93.8 0.0 collective-permute-done.3
  93.8 0.0 copy-done.10
  93.8 0.1 add_convert_fusion.3
  93.9 0.8 collective-permute-start.4
  94.7 1.5 collective-permute-start
  96.1 0.0 collective-permute-done.2
  96.1 0.0 copy-done.9
  96.1 0.1 add_convert_fusion.2
  96.2 0.4 collective-permute-start.5
  96.6 0.0 copy-done.12
  96.6 1.4 collective-permute-start.11
  98.0 0.0 collective-permute-done.1
  98.0 9.8 %collective-permute-done.4.end_ref = bf16[4,256,128]{2,1,0:T(8,128)(2,1)S(1)} collective-permute-done((bf16[4,256,128]{2,1,0:T(8,128)(2,1)S(1)}, bf16[4,256,128]{2,1,0:T(8,128)(2,1)S(1)}, u32[]{:S(2)}, u32[]{:S(2)}) %collective-permute-start.4) | collective-permute-done | bytes 262176 | tf_op jit(solution)/shard_map/ppermute | solution.py:153
  107.8 0.0 copy-done.8
  107.8 0.1 add_convert_fusion.1
  107.9 0.1 collective-permute-start.9
  108.0 0.0 collective-permute-done
  108.0 11.0 %collective-permute-done.5.end_ref = bf16[4,256,128]{2,1,0:T(8,128)(2,1)S(1)} collective-permute-done((bf16[4,256,128]{2,1,0:T(8,128)(2,1)S(1)}, bf16[4,256,128]{2,1,0:T(8,128)(2,1)S(1)}, u32[]{:S(2)}, u32[]{:S(2)}) %collective-permute-start.5) | collective-permute-done | bytes 262176 | tf_op jit(solution)/shard_map/ppermute | solution.py:153
  119.1 0.0 copy-done.7
  119.1 0.1 add_convert_fusion
  119.2 0.0 copy-done.13
  119.2 0.1 collective-permute-start.10
  119.3 0.0 copy-done.14
  119.3 1.4 collective-permute-start.8
  120.7 0.1 collective-permute-start.6
  120.8 0.0 collective-permute-done.11.near_ref
  120.8 2.1 %collective-permute-start.7 = (bf16[4,256,128]{2,1,0:T(8,128)(2,1)S(1)}, bf16[4,256,128]{2,1,0:T(8,128)(2,1)S(1)}, u32[]{:S(2)}, u32[]{:S(2)}) collective-permute-start(bf16[4,256,128]{2,1,0:T(8,128)(2,1)S(1)} %add_convert_fusion), channel_id=1, source_target_pairs={{0,128},{64,192},{128,0},{192,64},{1,129},{65,193},{129,1},{193,65... | collective-permute-start | bytes 786440 | tf_op jit(solution)/shard_map/ppermute | solution.py:153
  123.0 0.0 copy-done.6
  123.0 0.0 copy-done.11
  123.0 1.9 %finish.4.refs_0_ = bf16[16,256,128]{2,1,0:T(8,128)(2,1)} custom-call(bf16[16,256,128]{2,1,0:T(8,128)(2,1)} %get-tuple-element.41.mine_ref, bf16[4,256,128]{2,1,0:T(8,128)(2,1)} %copy-done.11, bf16[4,256,128]{2,1,0:T(8,128)(2,1)} %copy-done.6), custom_call_target="tpu_custom_call" | custom-call | bytes 32000000 | tf_op jit(solution)/shard_map/finish/pallas_call | solution.py:106
  124.9 4.7 %collective-permute-done.10.near_ref = bf16[4,256,128]{2,1,0:T(8,128)(2,1)S(1)} collective-permute-done((bf16[4,256,128]{2,1,0:T(8,128)(2,1)S(1)}, bf16[4,256,128]{2,1,0:T(8,128)(2,1)S(1)}, u32[]{:S(2)}, u32[]{:S(2)}) %collective-permute-start.10) | collective-permute-done | bytes 262176 | tf_op jit(solution)/shard_map/ppermute | solution.py:159
  129.6 0.0 copy-done
  129.6 0.7 copy-done.5
  130.3 1.9 %finish.5.refs_0_ = bf16[16,256,128]{2,1,0:T(8,128)(2,1)} custom-call(bf16[16,256,128]{2,1,0:T(8,128)(2,1)} %get-tuple-element.41.mine_ref, bf16[4,256,128]{2,1,0:T(8,128)(2,1)} %copy-done.5, bf16[4,256,128]{2,1,0:T(8,128)(2,1)} %copy-done, bf16[16,256,128]{2,1,0:T(8,128)(2,1)} %finish.4.refs_0_), custom_call_target="tpu_custom_call", output_to_operand_aliasing={{}: (3, {})} | custom-call | bytes 32000000 | tf_op jit(solution)/shard_map/finish/pallas_call | solution.py:106
  132.2 8.3 %collective-permute-done.8.near_ref = bf16[4,256,128]{2,1,0:T(8,128)(2,1)S(1)} collective-permute-done((bf16[4,256,128]{2,1,0:T(8,128)(2,1)S(1)}, bf16[4,256,128]{2,1,0:T(8,128)(2,1)S(1)}, u32[]{:S(2)}, u32[]{:S(2)}) %collective-permute-start.8) | collective-permute-done | bytes 262176 | tf_op jit(solution)/shard_map/ppermute | solution.py:159
  140.5 0.0 collective-permute-done.9.end_ref
  140.5 0.7 copy-done.4
  141.2 0.7 copy-done.1
  141.9 1.9 %finish.6.refs_0_ = bf16[16,256,128]{2,1,0:T(8,128)(2,1)} custom-call(bf16[16,256,128]{2,1,0:T(8,128)(2,1)} %get-tuple-element.41.mine_ref, bf16[4,256,128]{2,1,0:T(8,128)(2,1)} %copy-done.4, bf16[4,256,128]{2,1,0:T(8,128)(2,1)} %copy-done.1, bf16[16,256,128]{2,1,0:T(8,128)(2,1)} %finish.5.refs_0_), custom_call_target="tpu_custom_call", output_to_operand_aliasing={{}: (3, {})} | custom-call | bytes 32000000 | tf_op jit(solution)/shard_map/finish/pallas_call | solution.py:106
  143.8 2.3 %collective-permute-done.6.near_ref = bf16[4,256,128]{2,1,0:T(8,128)(2,1)S(1)} collective-permute-done((bf16[4,256,128]{2,1,0:T(8,128)(2,1)}, bf16[4,256,128]{2,1,0:T(8,128)(2,1)S(1)}, u32[]{:S(2)}, u32[]{:S(2)}) %collective-permute-start.6) | collective-permute-done | bytes 262176 | tf_op jit(solution)/shard_map/ppermute | solution.py:159
  146.1 0.3 collective-permute-done.7.end_ref
  146.5 0.4 copy-done.2
  146.8 0.7 copy-done.3
  147.5 1.9 %finish.7 = bf16[16,256,128]{2,1,0:T(8,128)(2,1)} custom-call(bf16[16,256,128]{2,1,0:T(8,128)(2,1)} %get-tuple-element.41.mine_ref, bf16[4,256,128]{2,1,0:T(8,128)(2,1)} %copy-done.2, bf16[4,256,128]{2,1,0:T(8,128)(2,1)} %copy-done.3, bf16[16,256,128]{2,1,0:T(8,128)(2,1)} %finish.6.refs_0_), custom_call_target="tpu_custom_call", output_to_operand_aliasing={{}: (3, {})} | custom-call | bytes 32000000 | tf_op jit(solution)/shard_map/finish/pallas_call | solution.py:106
  (13 shorter events, 0.0 us)
Async XLA Ops:
  4.5 53.4 %all-to-all-start = ((bf16[64,2,4,16,128]{4,3,2,1,0:T(8,128)(2,1)}), bf16[64,2,4,16,128]{4,3,2,1,0:T(8,128)(2,1)S(1)}, u32[]{:S(2)}, u32[]{:S(2)}) async-start(bf16[64,2,4,16,128]{4,3,2,1,0:T(8,128)(2,1)} %make_parts.1), calls=%async_computation | async-start | bytes 4194304 | tf_op jit(solution)/shard_map/all_to_all | solution.py:130
  62.3 31.6 %collective-permute-start.3 = (bf16[4,256,128]{2,1,0:T(8,128)(2,1)}, bf16[4,256,128]{2,1,0:T(8,128)(2,1)S(1)}, u32[]{:S(2)}, u32[]{:S(2)}) collective-permute-start(bf16[4,256,128]{2,1,0:T(8,128)(2,1)} %get-tuple-element.47), channel_id=1, source_target_pairs={{0,64},{64,0},{128,192},{192,128},{1,65},{65,1},{129,193},{193,129... | collective-permute-start | bytes 786440 | tf_op jit(solution)/shard_map/ppermute | solution.py:143
  83.4 12.7 %collective-permute-start.2 = (bf16[4,256,128]{2,1,0:T(8,128)(2,1)}, bf16[4,256,128]{2,1,0:T(8,128)(2,1)S(1)}, u32[]{:S(2)}, u32[]{:S(2)}) collective-permute-start(bf16[4,256,128]{2,1,0:T(8,128)(2,1)} %get-tuple-element.46), channel_id=1, source_target_pairs={{0,64},{64,0},{128,192},{192,128},{1,65},{65,1},{129,193},{193,129... | collective-permute-start | bytes 786440 | tf_op jit(solution)/shard_map/ppermute | solution.py:143
  89.1 8.9 %collective-permute-start.1 = (bf16[4,256,128]{2,1,0:T(8,128)(2,1)}, bf16[4,256,128]{2,1,0:T(8,128)(2,1)S(1)}, u32[]{:S(2)}, u32[]{:S(2)}) collective-permute-start(bf16[4,256,128]{2,1,0:T(8,128)(2,1)} %get-tuple-element.45), channel_id=1, source_target_pairs={{0,64},{64,0},{128,192},{192,128},{1,65},{65,1},{129,193},{193,129... | collective-permute-start | bytes 786440 | tf_op jit(solution)/shard_map/ppermute | solution.py:143
  90.5 3.3 %copy-start.10 = (bf16[4,256,128]{2,1,0:T(8,128)(2,1)S(1)}, bf16[4,256,128]{2,1,0:T(8,128)(2,1)}, u32[]{:S(2)}) copy-start(bf16[4,256,128]{2,1,0:T(8,128)(2,1)} %get-tuple-element.32) | copy-start | bytes 786436
  90.5 5.6 %copy-start.9 = (bf16[4,256,128]{2,1,0:T(8,128)(2,1)S(1)}, bf16[4,256,128]{2,1,0:T(8,128)(2,1)}, u32[]{:S(2)}) copy-start(bf16[4,256,128]{2,1,0:T(8,128)(2,1)} %get-tuple-element.35) | copy-start | bytes 786436
  90.5 6.0 %copy-start.12 = (bf16[4,256,128]{2,1,0:T(8,128)(2,1)S(1)}, bf16[4,256,128]{2,1,0:T(8,128)(2,1)}, u32[]{:S(2)}) copy-start(bf16[4,256,128]{2,1,0:T(8,128)(2,1)} %get-tuple-element.58) | copy-start | bytes 786436
  90.5 17.3 %copy-start.8 = (bf16[4,256,128]{2,1,0:T(8,128)(2,1)S(1)}, bf16[4,256,128]{2,1,0:T(8,128)(2,1)}, u32[]{:S(2)}) copy-start(bf16[4,256,128]{2,1,0:T(8,128)(2,1)} %get-tuple-element.38) | copy-start | bytes 786436
  93.8 25.3 %copy-start.7 = (bf16[4,256,128]{2,1,0:T(8,128)(2,1)S(1)}, bf16[4,256,128]{2,1,0:T(8,128)(2,1)}, u32[]{:S(2)}) copy-start(bf16[4,256,128]{2,1,0:T(8,128)(2,1)} %get-tuple-element.43) | copy-start | bytes 786436
  93.8 25.4 %copy-start.13 = (bf16[4,256,128]{2,1,0:T(8,128)(2,1)S(1)}, bf16[4,256,128]{2,1,0:T(8,128)(2,1)}, u32[]{:S(2)}) copy-start(bf16[4,256,128]{2,1,0:T(8,128)(2,1)} %get-tuple-element.56) | copy-start | bytes 786436
  93.8 25.5 %copy-start.14 = (bf16[4,256,128]{2,1,0:T(8,128)(2,1)S(1)}, bf16[4,256,128]{2,1,0:T(8,128)(2,1)}, u32[]{:S(2)}) copy-start(bf16[4,256,128]{2,1,0:T(8,128)(2,1)} %get-tuple-element.54) | copy-start | bytes 786436
  93.9 13.9 %collective-permute-start.4 = (bf16[4,256,128]{2,1,0:T(8,128)(2,1)S(1)}, bf16[4,256,128]{2,1,0:T(8,128)(2,1)S(1)}, u32[]{:S(2)}, u32[]{:S(2)}) collective-permute-start(bf16[4,256,128]{2,1,0:T(8,128)(2,1)S(1)} %add_convert_fusion.3), channel_id=1, source_target_pairs={{0,128},{64,192},{128,0},{192,64},{1,129},{65,193},{129,1},{193,65... | collective-permute-start | bytes 786440 | tf_op jit(solution)/shard_map/ppermute | solution.py:153
  94.7 13.4 %collective-permute-start = (bf16[4,256,128]{2,1,0:T(8,128)(2,1)}, bf16[4,256,128]{2,1,0:T(8,128)(2,1)S(1)}, u32[]{:S(2)}, u32[]{:S(2)}) collective-permute-start(bf16[4,256,128]{2,1,0:T(8,128)(2,1)} %get-tuple-element.44), channel_id=1, source_target_pairs={{0,64},{64,0},{128,192},{192,128},{1,65},{65,1},{129,193},{193,129... | collective-permute-start | bytes 786440 | tf_op jit(solution)/shard_map/ppermute | solution.py:143
  96.2 22.9 %collective-permute-start.5 = (bf16[4,256,128]{2,1,0:T(8,128)(2,1)S(1)}, bf16[4,256,128]{2,1,0:T(8,128)(2,1)S(1)}, u32[]{:S(2)}, u32[]{:S(2)}) collective-permute-start(bf16[4,256,128]{2,1,0:T(8,128)(2,1)S(1)} %add_convert_fusion.2), channel_id=1, source_target_pairs={{0,128},{64,192},{128,0},{192,64},{1,129},{65,193},{129,1},{193,65... | collective-permute-start | bytes 786440 | tf_op jit(solution)/shard_map/ppermute | solution.py:153
  96.6 24.3 %collective-permute-start.11 = (bf16[4,256,128]{2,1,0:T(8,128)(2,1)S(1)}, bf16[4,256,128]{2,1,0:T(8,128)(2,1)S(1)}, u32[]{:S(2)}, u32[]{:S(2)}) collective-permute-start(bf16[4,256,128]{2,1,0:T(8,128)(2,1)S(1)} %copy-done.12), channel_id=1, source_target_pairs={{0,64},{64,0},{128,192},{192,128},{1,65},{65,1},{129,193},{193,129... | collective-permute-start | bytes 786440 | tf_op jit(solution)/shard_map/ppermute | solution.py:159
  107.8 15.1 %copy-start.6 = (bf16[4,256,128]{2,1,0:T(8,128)(2,1)}, bf16[4,256,128]{2,1,0:T(8,128)(2,1)S(1)}, u32[]{:S(2)}) copy-start(bf16[4,256,128]{2,1,0:T(8,128)(2,1)S(1)} %collective-permute-done.4.end_ref) | copy-start | bytes 786436
  107.9 32.6 %collective-permute-start.9 = (bf16[4,256,128]{2,1,0:T(8,128)(2,1)S(1)}, bf16[4,256,128]{2,1,0:T(8,128)(2,1)S(1)}, u32[]{:S(2)}, u32[]{:S(2)}) collective-permute-start(bf16[4,256,128]{2,1,0:T(8,128)(2,1)S(1)} %add_convert_fusion.1), channel_id=1, source_target_pairs={{0,128},{64,192},{128,0},{192,64},{1,129},{65,193},{129,1},{193,65... | collective-permute-start | bytes 786440 | tf_op jit(solution)/shard_map/ppermute | solution.py:153
  119.1 10.5 %copy-start = (bf16[4,256,128]{2,1,0:T(8,128)(2,1)}, bf16[4,256,128]{2,1,0:T(8,128)(2,1)S(1)}, u32[]{:S(2)}) copy-start(bf16[4,256,128]{2,1,0:T(8,128)(2,1)S(1)} %collective-permute-done.5.end_ref) | copy-start | bytes 786436
  119.2 10.4 %collective-permute-start.10 = (bf16[4,256,128]{2,1,0:T(8,128)(2,1)S(1)}, bf16[4,256,128]{2,1,0:T(8,128)(2,1)S(1)}, u32[]{:S(2)}, u32[]{:S(2)}) collective-permute-start(bf16[4,256,128]{2,1,0:T(8,128)(2,1)S(1)} %copy-done.13), channel_id=1, source_target_pairs={{0,64},{64,0},{128,192},{192,128},{1,65},{65,1},{129,193},{193,129... | collective-permute-start | bytes 786440 | tf_op jit(solution)/shard_map/ppermute | solution.py:159
  119.3 21.2 %collective-permute-start.8 = (bf16[4,256,128]{2,1,0:T(8,128)(2,1)S(1)}, bf16[4,256,128]{2,1,0:T(8,128)(2,1)S(1)}, u32[]{:S(2)}, u32[]{:S(2)}) collective-permute-start(bf16[4,256,128]{2,1,0:T(8,128)(2,1)S(1)} %copy-done.14), channel_id=1, source_target_pairs={{0,64},{64,0},{128,192},{192,128},{1,65},{65,1},{129,193},{193,129... | collective-permute-start | bytes 786440 | tf_op jit(solution)/shard_map/ppermute | solution.py:159
  120.7 25.4 %collective-permute-start.6 = (bf16[4,256,128]{2,1,0:T(8,128)(2,1)}, bf16[4,256,128]{2,1,0:T(8,128)(2,1)S(1)}, u32[]{:S(2)}, u32[]{:S(2)}) collective-permute-start(bf16[4,256,128]{2,1,0:T(8,128)(2,1)} %get-tuple-element.52), channel_id=1, source_target_pairs={{0,64},{64,0},{128,192},{192,128},{1,65},{65,1},{129,193},{193,129... | collective-permute-start | bytes 786440 | tf_op jit(solution)/shard_map/ppermute | solution.py:159
  120.8 2.1 %copy-start.11 = (bf16[4,256,128]{2,1,0:T(8,128)(2,1)}, bf16[4,256,128]{2,1,0:T(8,128)(2,1)S(1)}, u32[]{:S(2)}) copy-start(bf16[4,256,128]{2,1,0:T(8,128)(2,1)S(1)} %collective-permute-done.11.near_ref) | copy-start | bytes 786436
  120.8 25.6 %collective-permute-start.7 = (bf16[4,256,128]{2,1,0:T(8,128)(2,1)S(1)}, bf16[4,256,128]{2,1,0:T(8,128)(2,1)S(1)}, u32[]{:S(2)}, u32[]{:S(2)}) collective-permute-start(bf16[4,256,128]{2,1,0:T(8,128)(2,1)S(1)} %add_convert_fusion), channel_id=1, source_target_pairs={{0,128},{64,192},{128,0},{192,64},{1,129},{65,193},{129,1},{193,65... | collective-permute-start | bytes 786440 | tf_op jit(solution)/shard_map/ppermute | solution.py:153
  129.6 0.7 copy-start.5
  140.5 0.7 copy-start.4
  141.2 0.7 copy-start.1
  146.1 0.7 copy-start.2
  146.8 0.7 copy-start.3

commit v4 on v3

--- a/solution.py
+++ b/solution.py
@@ -111,6 +111,7 @@
         out_shape=jax.ShapeDtypeStruct(mine.shape, mine.dtype),
         input_output_aliases={3: 0} if whole else {},
         name="finish",
+        compiler_params=pltpu.CompilerParams(vmem_limit_bytes=32000000),
         cost_estimate=pl.CostEstimate(flops=0, bytes_accessed=FINISH_BYTES * slots, transcendentals=0),
     )(mine, near, end, *whole)
 

time: 152 us -> 149 us (0.980)
  waiting for transfers between devices: 74.3 us -> 79.7 us
  Pallas kernels: 24.8 us -> 20.1 us
  local copies, waits for them, and re-layouts: 8.23 us -> 5.09 us
    ppermute x4, waiting for transfers between devices: 15.2 us -> 20.9 us  [per_device(): out = (finish(mine, lax.ppermute(near, 'lat', one), end, first, out),)]
    pallas_call x4, Pallas kernels: 7.64 us -> 3.08 us  [finish(): pl.pallas_call(final_kernel, grid=(slots // step,), in_specs=[every_spec,...]
    unnamed x30 -> x20, local copies, waits for them, and re-layouts: 3.26 us -> 0.04 us
  transfers between devices with their start and end apart: 13 -> 13, of which waited for: 7 -> 6; matrix products, arithmetic and copies ran while one was open for 3% -> 3% of each run, Pallas kernels for 10% -> 8%
where the time goes in v4:
time: 149 us; the launch traced here: 147 us
  waiting for transfers between devices  79.7 us (53%)
  starting transfers between devices  41.7 us (28%)
  Pallas kernels  20.1 us (13%)
  local copies, waits for them, and re-layouts  5.09 us (3%)
    all_to_all x1, waiting for transfers between devices, per_device(): got = lax.all_to_all(sent, 'wave', split_axis=0, concat_axis=0, tiled=True)  37.8 us
    ppermute x4, waiting for transfers between devices, per_device(): ends.append(lax.ppermute(pair, 'lat', two))  21 us
    ppermute x4, waiting for transfers between devices, per_device(): out = (finish(mine, lax.ppermute(near, 'lat', one), end, first, out),)  20.9 us
    ppermute x4, starting transfers between devices, per_device(): crosses.append(lax.ppermute(cross, 'lat', one))  19.7 us
    all_to_all x1, starting transfers between devices, per_device(): got = lax.all_to_all(sent, 'wave', split_axis=0, concat_axis=0, tiled=True)  15.6 us
    pallas_call x4, Pallas kernels, band_sums(): pl.pallas_call(band_kernel, grid_spec=pltpu.PrefetchScalarGridSpec(num_sc...  12.6 us
    transpose x8, local copies, waits for them, and re-layouts, per_device(): jnp.transpose(rows, (1, 3, 0, 2, 4))  5.05 us
    pallas_call x1, Pallas kernels, make_parts(): pl.pallas_call(functools.partial(parts_kernel, groups, width), out_shape=...  4.43 us
  transfers between devices with their start and end apart: 13, of which 6 were waited for; matrix products, arithmetic and copies ran while one was open for 3% of the time, Pallas kernels for 8%

profile of v4, /device:TPU:1, one launch (start us, length us, event | category | flops | bytes accessed | tf_op | source)
XLA Modules:
  0.0 147.0 jit_solution(15170775778523171678)
XLA Ops:
  0.0 4.4 %make_parts.1 = bf16[64,2,4,16,128]{4,3,2,1,0:T(8,128)(2,1)} custom-call(s32[4]{0:T(128)} %points_ref.1, s32[1024]{0:T(1024)} %table_ref.1, bf16[2,4,1024,128]{3,2,1,0:T(8,128)(2,1)} %fourier_ref.1), custom_call_target="tpu_custom_call" | custom-call | tf_op jit(solution)/shard_map/make_parts/pallas_call | solution.py:35
  4.4 15.6 %all-to-all-start = ((bf16[64,2,4,16,128]{4,3,2,1,0:T(8,128)(2,1)}), bf16[64,2,4,16,128]{4,3,2,1,0:T(8,128)(2,1)S(1)}, u32[]{:S(2)}, u32[]{:S(2)}) async-start(bf16[64,2,4,16,128]{4,3,2,1,0:T(8,128)(2,1)} %make_parts.1), calls=%async_computation | async-start | bytes 4194304 | tf_op jit(solution)/shard_map/all_to_all | solution.py:131
  20.1 37.8 %all-to-all-done = bf16[64,2,4,16,128]{4,3,2,1,0:T(8,128)(2,1)S(1)} async-done(((bf16[64,2,4,16,128]{4,3,2,1,0:T(8,128)(2,1)}), bf16[64,2,4,16,128]{4,3,2,1,0:T(8,128)(2,1)S(1)}, u32[]{:S(2)}, u32[]{:S(2)}) %all-to-all-start) | async-done | bytes 2097184 | tf_op jit(solution)/shard_map/all_to_all | solution.py:131
  57.9 0.2 slice_bitcast_fusion
  58.1 1.0 copy.11
  59.1 3.1 %band_sums.4 = (bf16[16,256,128]{2,1,0:T(8,128)(2,1)}, bf16[4,256,128]{2,1,0:T(8,128)(2,1)}, bf16[4,256,128]{2,1,0:T(8,128)(2,1)}, bf16[4,256,128]{2,1,0:T(8,128)(2,1)}) custom-call(s32[1]{0:T(128)} %bitcast.me_ref, bf16[2,4,256,128]{3,2,1,0:T(8,128)(2,1)} %bitcast.16, bf16[16,256,1024]{2,1,0:T(8,128)(2,1)} %legendre_ref.7), custom_call_target="tpu_custom_call" | custom-call | flops 268435456 | bytes 2097152 | tf_op jit(solution)/shard_map/band_sums/pallas_call | solution.py:72
  62.2 16.7 %collective-permute-start.3 = (bf16[4,256,128]{2,1,0:T(8,128)(2,1)}, bf16[4,256,128]{2,1,0:T(8,128)(2,1)S(1)}, u32[]{:S(2)}, u32[]{:S(2)}) collective-permute-start(bf16[4,256,128]{2,1,0:T(8,128)(2,1)} %get-tuple-element.47), channel_id=1, source_target_pairs={{0,64},{64,0},{128,192},{192,128},{1,65},{65,1},{129,193},{193,129... | collective-permute-start | bytes 786440 | tf_op jit(solution)/shard_map/ppermute | solution.py:144
  78.9 0.3 slice_bitcast_fusion.3
  79.2 1.0 copy.12
  80.3 3.1 %band_sums.5 = (bf16[16,256,128]{2,1,0:T(8,128)(2,1)}, bf16[4,256,128]{2,1,0:T(8,128)(2,1)}, bf16[4,256,128]{2,1,0:T(8,128)(2,1)}, bf16[4,256,128]{2,1,0:T(8,128)(2,1)}) custom-call(s32[1]{0:T(128)} %bitcast.me_ref, bf16[2,4,256,128]{3,2,1,0:T(8,128)(2,1)} %bitcast.14, bf16[16,256,1024]{2,1,0:T(8,128)(2,1)} %legendre_ref.7, ...), custom_call_target="tpu_custom_call", output_to_operand_aliasing={{0}: (3, {})} | custom-call | flops 268435456 | bytes 2097152 | tf_op jit(solution)/shard_map/band_sums/pallas_call | solution.py:72
  83.4 0.1 collective-permute-start.2
  83.4 0.2 slice_bitcast_fusion.2
  83.7 1.0 copy.13
  84.7 3.1 %band_sums.6 = (bf16[16,256,128]{2,1,0:T(8,128)(2,1)}, bf16[4,256,128]{2,1,0:T(8,128)(2,1)}, bf16[4,256,128]{2,1,0:T(8,128)(2,1)}, bf16[4,256,128]{2,1,0:T(8,128)(2,1)}) custom-call(s32[1]{0:T(128)} %bitcast.me_ref, bf16[2,4,256,128]{3,2,1,0:T(8,128)(2,1)} %bitcast.15, bf16[16,256,1024]{2,1,0:T(8,128)(2,1)} %legendre_ref.7, ...), custom_call_target="tpu_custom_call", output_to_operand_aliasing={{0}: (3, {})} | custom-call | flops 268435456 | bytes 2097152 | tf_op jit(solution)/shard_map/band_sums/pallas_call | solution.py:72
  87.8 0.0 copy-start.9
  87.8 0.3 slice_bitcast_fusion.1
  88.1 1.0 copy.14
  89.1 0.0 copy-done.9
  89.1 1.5 collective-permute-start.1
  90.6 0.0 copy-start.4
  90.6 0.0 copy-start.3
  90.6 0.0 copy-start.5
  90.6 3.2 %band_sums.7 = (bf16[16,256,128]{2,1,0:T(8,128)(2,1)}, bf16[4,256,128]{2,1,0:T(8,128)(2,1)}, bf16[4,256,128]{2,1,0:T(8,128)(2,1)}, bf16[4,256,128]{2,1,0:T(8,128)(2,1)}) custom-call(s32[1]{0:T(128)} %bitcast.me_ref, bf16[2,4,256,128]{3,2,1,0:T(8,128)(2,1)} %bitcast.13, bf16[16,256,1024]{2,1,0:T(8,128)(2,1)} %legendre_ref.7, ...), custom_call_target="tpu_custom_call", output_to_operand_aliasing={{0}: (3, {})} | custom-call | flops 268435456 | bytes 2097152 | tf_op jit(solution)/shard_map/band_sums/pallas_call | solution.py:72
  93.8 0.0 copy-start.7
  93.8 0.0 copy-start.8
  93.8 0.0 copy-start
  93.8 0.0 collective-permute-done.3
  93.9 0.0 copy-done.4
  93.9 0.1 add_convert_fusion.3
  93.9 0.7 collective-permute-start.4
  94.7 1.5 collective-permute-start
  96.1 0.0 collective-permute-done.2
  96.1 0.0 copy-done.3
  96.1 0.1 add_convert_fusion.2
  96.2 0.4 collective-permute-start.5
  96.6 0.0 copy-done.5
  96.6 1.4 collective-permute-start.11
  98.0 0.0 collective-permute-done.1
  98.0 9.9 %collective-permute-done.4.end_ref = bf16[4,256,128]{2,1,0:T(8,128)(2,1)S(1)} collective-permute-done((bf16[4,256,128]{2,1,0:T(8,128)(2,1)S(1)}, bf16[4,256,128]{2,1,0:T(8,128)(2,1)S(1)}, u32[]{:S(2)}, u32[]{:S(2)}) %collective-permute-start.4) | collective-permute-done | bytes 262176 | tf_op jit(solution)/shard_map/ppermute | solution.py:154
  108.0 0.0 copy-done.2
  108.0 0.1 add_convert_fusion.1
  108.1 0.1 collective-permute-start.9
  108.2 0.0 collective-permute-done
  108.2 11.0 %collective-permute-done.5.end_ref = bf16[4,256,128]{2,1,0:T(8,128)(2,1)S(1)} collective-permute-done((bf16[4,256,128]{2,1,0:T(8,128)(2,1)S(1)}, bf16[4,256,128]{2,1,0:T(8,128)(2,1)S(1)}, u32[]{:S(2)}, u32[]{:S(2)}) %collective-permute-start.5) | collective-permute-done | bytes 262176 | tf_op jit(solution)/shard_map/ppermute | solution.py:154
  119.2 0.0 copy-done.1
  119.2 0.1 add_convert_fusion
  119.3 0.0 copy-done.6
  119.3 0.1 collective-permute-start.10
  119.4 0.0 copy-done.7
  119.4 1.4 collective-permute-start.8
  120.9 0.0 copy-done.8
  120.9 0.1 collective-permute-start.6
  121.0 0.0 collective-permute-done.11.near_ref
  121.0 2.1 %collective-permute-start.7 = (bf16[4,256,128]{2,1,0:T(8,128)(2,1)S(1)}, bf16[4,256,128]{2,1,0:T(8,128)(2,1)S(1)}, u32[]{:S(2)}, u32[]{:S(2)}) collective-permute-start(bf16[4,256,128]{2,1,0:T(8,128)(2,1)S(1)} %add_convert_fusion), channel_id=1, source_target_pairs={{0,128},{64,192},{128,0},{192,64},{1,129},{65,193},{129,1},{193,65... | collective-permute-start | bytes 786440 | tf_op jit(solution)/shard_map/ppermute | solution.py:154
  123.1 0.0 copy-done
  123.1 0.8 finish.4.refs_0_
  123.9 5.6 %collective-permute-done.10.near_ref = bf16[4,256,128]{2,1,0:T(8,128)(2,1)S(1)} collective-permute-done((bf16[4,256,128]{2,1,0:T(8,128)(2,1)S(1)}, bf16[4,256,128]{2,1,0:T(8,128)(2,1)S(1)}, u32[]{:S(2)}, u32[]{:S(2)}) %collective-permute-start.10) | collective-permute-done | bytes 262176 | tf_op jit(solution)/shard_map/ppermute | solution.py:160
  129.4 0.8 finish.5.refs_0_
  130.2 10.5 %collective-permute-done.8.near_ref = bf16[4,256,128]{2,1,0:T(8,128)(2,1)S(1)} collective-permute-done((bf16[4,256,128]{2,1,0:T(8,128)(2,1)S(1)}, bf16[4,256,128]{2,1,0:T(8,128)(2,1)S(1)}, u32[]{:S(2)}, u32[]{:S(2)}) %collective-permute-start.8) | collective-permute-done | bytes 262176 | tf_op jit(solution)/shard_map/ppermute | solution.py:160
  140.6 0.0 collective-permute-done.9.end_ref
  140.6 0.8 finish.6.refs_0_
  141.4 4.8 %collective-permute-done.6.near_ref = bf16[4,256,128]{2,1,0:T(8,128)(2,1)S(1)} collective-permute-done((bf16[4,256,128]{2,1,0:T(8,128)(2,1)S(1)}, bf16[4,256,128]{2,1,0:T(8,128)(2,1)S(1)}, u32[]{:S(2)}, u32[]{:S(2)}) %collective-permute-start.6) | collective-permute-done | bytes 262176 | tf_op jit(solution)/shard_map/ppermute | solution.py:160
  146.2 0.0 collective-permute-done.7.end_ref
  146.3 0.8 finish.7
  (3 shorter events, 0.0 us)
Async XLA Ops:
  4.4 53.4 %all-to-all-start = ((bf16[64,2,4,16,128]{4,3,2,1,0:T(8,128)(2,1)}), bf16[64,2,4,16,128]{4,3,2,1,0:T(8,128)(2,1)S(1)}, u32[]{:S(2)}, u32[]{:S(2)}) async-start(bf16[64,2,4,16,128]{4,3,2,1,0:T(8,128)(2,1)} %make_parts.1), calls=%async_computation | async-start | bytes 4194304 | tf_op jit(solution)/shard_map/all_to_all | solution.py:131
  62.2 31.6 %collective-permute-start.3 = (bf16[4,256,128]{2,1,0:T(8,128)(2,1)}, bf16[4,256,128]{2,1,0:T(8,128)(2,1)S(1)}, u32[]{:S(2)}, u32[]{:S(2)}) collective-permute-start(bf16[4,256,128]{2,1,0:T(8,128)(2,1)} %get-tuple-element.47), channel_id=1, source_target_pairs={{0,64},{64,0},{128,192},{192,128},{1,65},{65,1},{129,193},{193,129... | collective-permute-start | bytes 786440 | tf_op jit(solution)/shard_map/ppermute | solution.py:144
  83.4 12.8 %collective-permute-start.2 = (bf16[4,256,128]{2,1,0:T(8,128)(2,1)}, bf16[4,256,128]{2,1,0:T(8,128)(2,1)S(1)}, u32[]{:S(2)}, u32[]{:S(2)}) collective-permute-start(bf16[4,256,128]{2,1,0:T(8,128)(2,1)} %get-tuple-element.46), channel_id=1, source_target_pairs={{0,64},{64,0},{128,192},{192,128},{1,65},{65,1},{129,193},{193,129... | collective-permute-start | bytes 786440 | tf_op jit(solution)/shard_map/ppermute | solution.py:144
  87.8 1.3 copy-start.9
  89.1 8.9 %collective-permute-start.1 = (bf16[4,256,128]{2,1,0:T(8,128)(2,1)S(1)}, bf16[4,256,128]{2,1,0:T(8,128)(2,1)S(1)}, u32[]{:S(2)}, u32[]{:S(2)}) collective-permute-start(bf16[4,256,128]{2,1,0:T(8,128)(2,1)S(1)} %copy-done.9), channel_id=1, source_target_pairs={{0,64},{64,0},{128,192},{192,128},{1,65},{65,1},{129,193},{193,129... | collective-permute-start | bytes 786440 | tf_op jit(solution)/shard_map/ppermute | solution.py:144
  90.6 3.3 %copy-start.4 = (bf16[4,256,128]{2,1,0:T(8,128)(2,1)S(1)}, bf16[4,256,128]{2,1,0:T(8,128)(2,1)}, u32[]{:S(2)}) copy-start(bf16[4,256,128]{2,1,0:T(8,128)(2,1)} %get-tuple-element.32) | copy-start | bytes 786436
  90.6 5.6 %copy-start.3 = (bf16[4,256,128]{2,1,0:T(8,128)(2,1)S(1)}, bf16[4,256,128]{2,1,0:T(8,128)(2,1)}, u32[]{:S(2)}) copy-start(bf16[4,256,128]{2,1,0:T(8,128)(2,1)} %get-tuple-element.35) | copy-start | bytes 786436
  90.6 6.0 %copy-start.5 = (bf16[4,256,128]{2,1,0:T(8,128)(2,1)S(1)}, bf16[4,256,128]{2,1,0:T(8,128)(2,1)}, u32[]{:S(2)}) copy-start(bf16[4,256,128]{2,1,0:T(8,128)(2,1)} %get-tuple-element.58) | copy-start | bytes 786436
  90.6 17.4 %copy-start.2 = (bf16[4,256,128]{2,1,0:T(8,128)(2,1)S(1)}, bf16[4,256,128]{2,1,0:T(8,128)(2,1)}, u32[]{:S(2)}) copy-start(bf16[4,256,128]{2,1,0:T(8,128)(2,1)} %get-tuple-element.38) | copy-start | bytes 786436
  93.8 25.4 %copy-start.1 = (bf16[4,256,128]{2,1,0:T(8,128)(2,1)S(1)}, bf16[4,256,128]{2,1,0:T(8,128)(2,1)}, u32[]{:S(2)}) copy-start(bf16[4,256,128]{2,1,0:T(8,128)(2,1)} %get-tuple-element.43) | copy-start | bytes 786436
  93.8 25.5 %copy-start.6 = (bf16[4,256,128]{2,1,0:T(8,128)(2,1)S(1)}, bf16[4,256,128]{2,1,0:T(8,128)(2,1)}, u32[]{:S(2)}) copy-start(bf16[4,256,128]{2,1,0:T(8,128)(2,1)} %get-tuple-element.56) | copy-start | bytes 786436
  93.8 25.6 %copy-start.7 = (bf16[4,256,128]{2,1,0:T(8,128)(2,1)S(1)}, bf16[4,256,128]{2,1,0:T(8,128)(2,1)}, u32[]{:S(2)}) copy-start(bf16[4,256,128]{2,1,0:T(8,128)(2,1)} %get-tuple-element.54) | copy-start | bytes 786436
  93.8 27.0 %copy-start.8 = (bf16[4,256,128]{2,1,0:T(8,128)(2,1)S(1)}, bf16[4,256,128]{2,1,0:T(8,128)(2,1)}, u32[]{:S(2)}) copy-start(bf16[4,256,128]{2,1,0:T(8,128)(2,1)} %get-tuple-element.52) | copy-start | bytes 786436
  93.8 29.2 %copy-start = (bf16[16,256,128]{2,1,0:T(8,128)(2,1)S(1)}, bf16[16,256,128]{2,1,0:T(8,128)(2,1)}, u32[]{:S(2)}) copy-start(bf16[16,256,128]{2,1,0:T(8,128)(2,1)} %get-tuple-element.41.mine_ref) | copy-start | bytes 3145732
  93.9 14.0 %collective-permute-start.4 = (bf16[4,256,128]{2,1,0:T(8,128)(2,1)S(1)}, bf16[4,256,128]{2,1,0:T(8,128)(2,1)S(1)}, u32[]{:S(2)}, u32[]{:S(2)}) collective-permute-start(bf16[4,256,128]{2,1,0:T(8,128)(2,1)S(1)} %add_convert_fusion.3), channel_id=1, source_target_pairs={{0,128},{64,192},{128,0},{192,64},{1,129},{65,193},{129,1},{193,65... | collective-permute-start | bytes 786440 | tf_op jit(solution)/shard_map/ppermute | solution.py:154
  94.7 13.5 %collective-permute-start = (bf16[4,256,128]{2,1,0:T(8,128)(2,1)}, bf16[4,256,128]{2,1,0:T(8,128)(2,1)S(1)}, u32[]{:S(2)}, u32[]{:S(2)}) collective-permute-start(bf16[4,256,128]{2,1,0:T(8,128)(2,1)} %get-tuple-element.44), channel_id=1, source_target_pairs={{0,64},{64,0},{128,192},{192,128},{1,65},{65,1},{129,193},{193,129... | collective-permute-start | bytes 786440 | tf_op jit(solution)/shard_map/ppermute | solution.py:144
  96.2 23.0 %collective-permute-start.5 = (bf16[4,256,128]{2,1,0:T(8,128)(2,1)S(1)}, bf16[4,256,128]{2,1,0:T(8,128)(2,1)S(1)}, u32[]{:S(2)}, u32[]{:S(2)}) collective-permute-start(bf16[4,256,128]{2,1,0:T(8,128)(2,1)S(1)} %add_convert_fusion.2), channel_id=1, source_target_pairs={{0,128},{64,192},{128,0},{192,64},{1,129},{65,193},{129,1},{193,65... | collective-permute-start | bytes 786440 | tf_op jit(solution)/shard_map/ppermute | solution.py:154
  96.6 24.4 %collective-permute-start.11 = (bf16[4,256,128]{2,1,0:T(8,128)(2,1)S(1)}, bf16[4,256,128]{2,1,0:T(8,128)(2,1)S(1)}, u32[]{:S(2)}, u32[]{:S(2)}) collective-permute-start(bf16[4,256,128]{2,1,0:T(8,128)(2,1)S(1)} %copy-done.5), channel_id=1, source_target_pairs={{0,64},{64,0},{128,192},{192,128},{1,65},{65,1},{129,193},{193,129... | collective-permute-start | bytes 786440 | tf_op jit(solution)/shard_map/ppermute | solution.py:160
  108.1 32.6 %collective-permute-start.9 = (bf16[4,256,128]{2,1,0:T(8,128)(2,1)S(1)}, bf16[4,256,128]{2,1,0:T(8,128)(2,1)S(1)}, u32[]{:S(2)}, u32[]{:S(2)}) collective-permute-start(bf16[4,256,128]{2,1,0:T(8,128)(2,1)S(1)} %add_convert_fusion.1), channel_id=1, source_target_pairs={{0,128},{64,192},{128,0},{192,64},{1,129},{65,193},{129,1},{193,65... | collective-permute-start | bytes 786440 | tf_op jit(solution)/shard_map/ppermute | solution.py:154
  119.3 10.1 %collective-permute-start.10 = (bf16[4,256,128]{2,1,0:T(8,128)(2,1)S(1)}, bf16[4,256,128]{2,1,0:T(8,128)(2,1)S(1)}, u32[]{:S(2)}, u32[]{:S(2)}) collective-permute-start(bf16[4,256,128]{2,1,0:T(8,128)(2,1)S(1)} %copy-done.6), channel_id=1, source_target_pairs={{0,64},{64,0},{128,192},{192,128},{1,65},{65,1},{129,193},{193,129... | collective-permute-start | bytes 786440 | tf_op jit(solution)/shard_map/ppermute | solution.py:160
  119.4 21.2 %collective-permute-start.8 = (bf16[4,256,128]{2,1,0:T(8,128)(2,1)S(1)}, bf16[4,256,128]{2,1,0:T(8,128)(2,1)S(1)}, u32[]{:S(2)}, u32[]{:S(2)}) collective-permute-start(bf16[4,256,128]{2,1,0:T(8,128)(2,1)S(1)} %copy-done.7), channel_id=1, source_target_pairs={{0,64},{64,0},{128,192},{192,128},{1,65},{65,1},{129,193},{193,129... | collective-permute-start | bytes 786440 | tf_op jit(solution)/shard_map/ppermute | solution.py:160
  120.9 25.4 %collective-permute-start.6 = (bf16[4,256,128]{2,1,0:T(8,128)(2,1)S(1)}, bf16[4,256,128]{2,1,0:T(8,128)(2,1)S(1)}, u32[]{:S(2)}, u32[]{:S(2)}) collective-permute-start(bf16[4,256,128]{2,1,0:T(8,128)(2,1)S(1)} %copy-done.8), channel_id=1, source_target_pairs={{0,64},{64,0},{128,192},{192,128},{1,65},{65,1},{129,193},{193,129... | collective-permute-start | bytes 786440 | tf_op jit(solution)/shard_map/ppermute | solution.py:160
  121.0 25.3 %collective-permute-start.7 = (bf16[4,256,128]{2,1,0:T(8,128)(2,1)S(1)}, bf16[4,256,128]{2,1,0:T(8,128)(2,1)S(1)}, u32[]{:S(2)}, u32[]{:S(2)}) collective-permute-start(bf16[4,256,128]{2,1,0:T(8,128)(2,1)S(1)} %add_convert_fusion), channel_id=1, source_target_pairs={{0,128},{64,192},{128,0},{192,64},{1,129},{65,193},{129,1},{193,65... | collective-permute-start | bytes 786440 | tf_op jit(solution)/shard_map/ppermute | solution.py:154
